TPU v7x, 256 devices: a whole 4x4x8 slice. The times are simulated.
256 devices in a mesh: aux: 32 (over z, y), occ: 8 (over x, core).
Axes of the slice: x: 4, y: 4, z: 8, core: 2. Of those that a mesh axis runs over, the one named last changes fastest.
Arguments:
- ints: bfloat16 [32, 16, 16, 16384], P(None, None, None, 'aux'), may hold values from -0.125 to 0.125
- blk_atoms: int32 [1024, 2], P('aux'), may hold values from 0 to 255
- blk_count: int32 [32], P('aux'), may hold values from 1 to 32, as said below
- occ_coeff: bfloat16 [1280, 4096], P(None, 'occ'), may hold values from -1.5 to 1.5
- vir_coeff: bfloat16 [4096, 3072], P(None, 'occ'), may hold values from -1.5 to 1.5
- batch_ids: int32 [8], replicated, may hold values from 0 to 1279, as said below
Outputs:
- pair_ints: float32 [8, 32, 96, 8, 96], P(None, 'aux', 'occ')
Inputs may be any that keep to these rules, and one draw needn't show every extreme that they name: `batch_ids`: the batch's orbitals are distinct, and the batch holds the last occupied orbital. `blk_count`: every owner has at least one live slot, and some owner has all 32 live. Slots of owner g name atoms within 2 * 256 // 32 (at least 2) atoms after atom g * 8, cyclically.
All inputs are finite; a program needn't handle non-finite values.
Results may differ from a plain program's by a relative error of at most 0.0017.
Values may be sent and summed in bfloat16 or wider, within the bound.
A program may use at most 128 MiB of HBM per device.

v0:
```python
import jax
import jax.numpy as jnp
from jax import lax
from jax.sharding import PartitionSpec as P


def half_transform(left_rows, right_rows, block_ints, live_count):
    half_ints = jnp.einsum(
        "ikm,kmnq->kinq", left_rows, block_ints, preferred_element_type=jnp.float32
    )
    slot_ids = jnp.arange(block_ints.shape[0], dtype=jnp.int32)
    half_ints = jnp.where((slot_ids < live_count)[:, None, None, None], half_ints, 0.0).astype(
        jnp.bfloat16
    )
    return jnp.einsum("knv,kinq->ivq", right_rows, half_ints, preferred_element_type=jnp.float32)


def on_device(ints, blk_atoms, blk_count, occ_coeff, vir_coeff, batch_ids):
    batch_size = batch_ids.shape[0]
    block_size = ints.shape[1]
    aux_local = ints.shape[3]
    picked = jnp.take(occ_coeff, batch_ids, axis=0)
    batch_coeff = lax.all_gather(picked, "occ", axis=1, tiled=True)
    atom_total = batch_coeff.shape[1] // block_size
    left_all = batch_coeff.reshape(batch_size, atom_total, block_size)[:, blk_atoms[:, 0], :]
    vir_local = vir_coeff.shape[1]
    right_all = vir_coeff.reshape(atom_total, block_size, vir_local)[blk_atoms[:, 1]]
    live_count = blk_count[0]
    summed = half_transform(left_all, right_all, ints, live_count)
    group_count = lax.axis_size("aux")
    vir_group = vir_local // group_count
    fitted = summed.astype(jnp.bfloat16).reshape(batch_size, group_count, vir_group, aux_local)
    regrouped = lax.all_to_all(
        lax.all_to_all(fitted, "aux", split_axis=1, concat_axis=3, tiled=True),
        "occ",
        split_axis=3,
        concat_axis=2,
        tiled=True,
    )
    group_rows = regrouped[:, 0]
    group_width = group_rows.shape[1]
    flat_rows = group_rows.reshape(batch_size * group_width, group_rows.shape[2])
    kept_rows = lax.psum_scatter(
        jnp.einsum("icq,xq->cix", group_rows, flat_rows, preferred_element_type=jnp.float32),
        "occ",
        scatter_dimension=0,
        tiled=True,
    )
    pair_ints = jnp.transpose(
        kept_rows.reshape(vir_group, batch_size, batch_size, group_width), (1, 0, 2, 3)
    )[:, None]
    return pair_ints


def solution(mesh):
    in_specs = (
        P(None, None, None, "aux"),
        P("aux", None),
        P("aux"),
        P(None, "occ"),
        P(None, "occ"),
        P(),
    )
    out_specs = P(None, "aux", "occ", None, None)
    return jax.shard_map(
        on_device, mesh=mesh, in_specs=in_specs, out_specs=out_specs, check_vma=False
    )
```

profile of v0, /device:TPU:8, one launch (start us, length us, event | category | flops | bytes accessed | tf_op | source)
XLA Modules:
  0.0 446.1 jit_solution(9911982256026092294)
XLA Ops:
  6.5 0.0 copy-start
  6.5 0.0 reduce-scatter.2.cloned.1.call-start
  6.5 0.8 compare_and_fusion
  7.4 0.8 compare_select_fusion.2
  8.8 0.8 fusion.17
  9.6 2.1 gather_fusion
  11.7 0.1 broadcast_select_fusion
  11.8 13.1 %all_gather.3 = bf16[8,4096]{1,0:T(8,128)(2,1)S(1)} all-gather(bf16[8,512]{1,0:T(8,128)(2,1)S(1)} %broadcast_select_fusion), channel_id=1, replica_groups=mesh['aux'=32,'occ'=8] {'occ'}, dimensions={1}, use_global_device_ids=true | all-gather | bytes 73728 | tf_op jit(solution)/shard_map/all_gather | solution.py:23
  24.8 1.2 reshape.23
  26.0 2.2 copy.29
  28.2 0.0 copy-done
  28.2 0.6 gather_fusion.2
  28.8 1.6 gather_fusion.1
  30.5 8.2 %select_convert_fusion = bf16[32,8,16,512]{3,1,2,0:T(8,128)(2,1)S(1)} fusion(pred[32]{0:T(512)(128)(4,1)S(1)} %iota_compare_fusion, bf16[32,16,16,512]{3,2,1,0:T(8,128)(2,1)} %param.6, bf16[32,8,16]{2,1,0:T(8,128)(2,1)S(1)} %gather_fusion.1), kind=kOutput, calls=%fused_computation.5 | convolution fusion | flops 71303168 | bytes 12591136 | tf_op jit(solution)/shard_map/ikm,kmnq->kinq/dot_general | solution.py:8
  38.7 2.2 fusion.4
  41.0 1.8 copy.32
  42.7 85.2 %all_to_all.33 = bf16[8,32,12,512]{3,0,2,1:T(8,128)(2,1)S(1)} all-to-all(bf16[8,32,12,512]{3,0,2,1:T(8,128)(2,1)S(1)} %bitcast.48), channel_id=1, replica_groups=mesh['aux'=32,'occ'=8] {'aux'}, dimensions={1} | all-to-all | bytes 6291456 | tf_op jit(solution)/shard_map/all_to_all | solution.py:34
  127.9 24.9 %copy.43 = bf16[8,1,12,32,512]{2,0,4,3,1:T(8,128)(2,1)} copy(bf16[8,1,12,32,512]{4,0,2,3,1:T(8,128)(2,1)S(1)} %bitcast.47) | data formatting | bytes 6291456 | tf_op jit(solution)/shard_map/all_to_all | solution.py:34
  152.7 75.3 %reshape.57 = bf16[8,2,98304]{2,1,0:T(2,128)(2,1)S(1)} reshape(bf16[16384,1,8,12]{3,2,1,0:T(8,128)(2,1)} %bitcast.43) | data formatting | bytes 6291456
  228.0 42.7 %all_to_all.34 = bf16[8,2,98304]{2,1,0:T(2,128)(2,1)} all-to-all(bf16[8,2,98304]{2,1,0:T(2,128)(2,1)S(1)} %reshape.57), channel_id=1, replica_groups=mesh['aux'=32,'occ'=8] {'occ'}, dimensions={0} | all-to-all | bytes 6291456 | tf_op jit(solution)/shard_map/all_to_all | solution.py:33
  270.8 82.2 %reshape.58 = bf16[16384,1,8,12]{3,2,1,0:T(8,128)(2,1)} reshape(bf16[8,2,98304]{2,1,0:T(2,128)(2,1)} %all_to_all.34) | data formatting | bytes 6291456
  353.0 26.8 %copy.44 = bf16[8,1,12,8,2048]{4,3,0,2,1:T(8,128)(2,1)S(1)} copy(bf16[8,1,12,8,2048]{2,0,4,3,1:T(8,128)(2,1)} %bitcast.44) | data formatting | bytes 6291456 | tf_op jit(solution)/shard_map/all_to_all | solution.py:33
  379.7 3.4 copy.37
  383.1 4.1 copy.36
  387.3 6.4 %reshape.55 = bf16[768,2048,1]{1,0,2:T(8,128)(2,1)} reshape(bf16[8,1,8,12,2048]{4,3,2,0,1:T(8,128)(2,1)} %copy.36) | data formatting | bytes 6291456 | tf_op jit(solution)/shard_map/reshape;squeeze | solution.py:42
  393.7 0.0 copy-start.1
  393.7 8.6 %fusion.11 = f32[96,8,768]{2,0,1:T(8,128)S(1)} fusion(bf16[768,2048,1]{1,0,2:T(8,128)(2,1)} %reshape.55, bf16[8,96,2048]{2,0,1:T(8,128)(2,1)} %bitcast.49), kind=kOutput, calls=%fused_computation.12 | convolution fusion | flops 2415919104 | bytes 8650752 | tf_op jit(solution)/shard_map/icq,xq->cix/dot_general | solution.py:44
  402.3 2.8 copy.39
  405.1 0.0 reduce-scatter.2.cloned.1.call-update
  405.1 31.7 %reduce-scatter.2.cloned.1.call-done = f32[12,8,768]{2,1,0:T(8,128)} async-done(((f32[96,8,768]{2,1,0:T(8,128)}), f32[12,8,768]{2,1,0:T(8,128)}) %reduce-scatter.2.cloned.1.call-update) | async-done | bytes 294928 | tf_op jit(solution)/shard_map/reduce_scatter | solution.py:43
  436.8 1.1 reshape.26
  438.0 0.8 copy.40
  438.8 0.0 copy-done.1
  (4 shorter events, 0.0 us)
Async XLA Ops:
  6.5 21.7 %copy-start = (bf16[4096,384]{1,0:T(8,128)(2,1)S(1)}, bf16[4096,384]{1,0:T(8,128)(2,1)}, u32[]{:S(2)}) copy-start(bf16[4096,384]{1,0:T(8,128)(2,1)} %param.10) | copy-start | bytes 9437188
  6.5 430.3 %reduce-scatter.2.cloned.1.call-start = ((), (), s32[]{:S(2)}) async-start(), calls=%async_computation.3 | async-start | bytes 2654208 | tf_op jit(solution)/shard_map/reduce_scatter | solution.py:43
  393.7 45.1 %copy-start.1 = (bf16[4096,384]{1,0:T(8,128)(2,1)S(1)}, bf16[4096,384]{1,0:T(8,128)(2,1)}, u32[]{:S(2)}) copy-start(bf16[4096,384]{1,0:T(8,128)(2,1)} %param.10) | copy-start | bytes 9437188
Sparse Core Ops, SparseCore 0:
  405.2 31.5 reduce-scatter.1
where the time goes:
time: 455 us; the launch traced here: 446 us
  local copies, waits for them, and re-layouts  237 us (52%)
  blocking collectives  141 us (31%)
  waiting for transfers between devices  31.7 us (7%)
  matrix products  19.1 us (4%)
  between operations  14.6 us (3%)
    unnamed x6, local copies, waits for them, and re-layouts  157 us
    all_to_all x1, blocking collectives, on_device(): lax.all_to_all(fitted, 'aux', split_axis=1, concat_axis=3, tiled=True)  85.2 us
    all_to_all x1, blocking collectives, on_device(): lax.all_to_all(lax.all_to_all(fitted, 'aux', split_axis=1, concat_axis=3,...  42.7 us
    all_to_all x3, local copies, waits for them, and re-layouts, on_device(): lax.all_to_all(lax.all_to_all(fitted, 'aux', split_axis=1, concat_axis=3,...  34.3 us
    reduce_scatter x1, waiting for transfers between devices, on_device(): lax.psum_scatter(jnp.einsum('icq,xq->cix', group_rows, flat_rows, preferr...  31.7 us
    all_to_all x1, local copies, waits for them, and re-layouts, on_device(): lax.all_to_all(fitted, 'aux', split_axis=1, concat_axis=3, tiled=True)  24.9 us
    all_gather x1, blocking collectives, on_device(): batch_coeff = lax.all_gather(picked, 'occ', axis=1, tiled=True)  13.1 us
  transfers between devices with their start and end apart: 1, of which 1 were waited for; matrix products, arithmetic and copies ran while one was open for 0% of the time, Pallas kernels for 0%

commit v1 on v0

v1 whole, which is shorter than its diff:
```python
import jax
import jax.numpy as jnp
from jax import lax
from jax.experimental import pallas as pl
from jax.experimental.pallas import tpu as pltpu
from jax.sharding import PartitionSpec as P

ROWS = 4


def fit_kernel(vir_ref, half_ref, place_ref, fit_ref):
    ranks = vir_ref.shape[0]
    wide = jnp.concatenate([vir_ref[a] for a in range(ranks)], axis=1)
    placed = jnp.dot(wide, place_ref[...], preferred_element_type=jnp.float32).astype(jnp.bfloat16)
    groups, owners, width = fit_ref.shape[0], fit_ref.shape[1], fit_ref.shape[2]
    span = groups * width
    for t in range(owners):
        summed = lax.dot_general(
            placed[:, span * t : span * (t + 1)],
            half_ref[t],
            (((0,), (0,)), ((), ())),
            preferred_element_type=jnp.float32,
        )
        for g in range(groups):
            fit_ref[g, t] = summed[width * g : width * (g + 1)].astype(jnp.bfloat16)


def gram_kernel(fit_ref, out_ref, rows, gram, sorted_rows):
    owners, width, lanes = fit_ref.shape
    batch = rows.shape[0] // width
    part = lanes // batch
    for o in range(owners // 2):
        for h in range(batch // 2):
            first = fit_ref[2 * o, :, 2 * part * h : 2 * part * (h + 1)]
            second = fit_ref[2 * o + 1, :, 2 * part * h : 2 * part * (h + 1)]
            cols = slice(2 * part * o, 2 * part * (o + 1))
            rows[width * 2 * h : width * (2 * h + 1), cols] = jnp.concatenate(
                [first[:, :part], second[:, :part]], axis=1
            )
            rows[width * (2 * h + 1) : width * (2 * h + 2), cols] = jnp.concatenate(
                [first[:, part:], second[:, part:]], axis=1
            )
    half = rows.shape[0] // 2
    for t in range(2):
        gram[half * t : half * (t + 1)] = lax.dot_general(
            rows[half * t : half * (t + 1)],
            rows[...],
            (((1,), (1,)), ((), ())),
            preferred_element_type=jnp.float32,
        )
    ranks = out_ref.shape[0]
    kept = width // ranks
    for a in range(ranks):
        for i in range(batch):
            sorted_rows[kept * i : kept * (i + 1)] = gram[
                width * i + kept * a : width * i + kept * (a + 1)
            ]
        out_ref[a] = sorted_rows[...].astype(jnp.bfloat16)


def on_device(ints, blk_atoms, blk_count, occ_coeff, vir_coeff, batch_ids):
    batch = batch_ids.shape[0]
    slots, block_size = ints.shape[0], ints.shape[1]
    aux_local = ints.shape[3]
    ranks = lax.axis_size("occ")
    group_count = lax.axis_size("aux")
    planes = group_count // ROWS
    owner, rank = lax.axis_index("aux"), lax.axis_index("occ")
    plane, row = owner // ROWS, owner % ROWS
    atom_total = vir_coeff.shape[0] // block_size
    step = atom_total // group_count
    window = 2 * step + 1
    depth = window * block_size
    part = aux_local // ranks
    vir_group = vir_coeff.shape[1] // group_count
    width = vir_group * ranks
    lane = 64

    with jax.named_scope("vir_rows"):
        cols = lax.dynamic_slice_in_dim(vir_coeff, plane * (ROWS * vir_group), ROWS * vir_group, 1)
        cols = jnp.pad(cols, ((0, 0), (0, lane - ROWS * vir_group)))
        stride = ROWS * step * block_size
        reach = stride * (planes - 1) + depth
        start = row * (step * block_size)
        longest = (ROWS - 1) * step * block_size + reach
        cols = jnp.concatenate([cols, cols[: longest - cols.shape[0]]], axis=0)
        cols = lax.dynamic_slice_in_dim(cols, start, reach, 0)
        vir_rows = jnp.concatenate(
            [cols[stride * z : stride * z + depth] for z in range(planes)], axis=1
        )
        vir_all = lax.all_gather(vir_rows, "occ", axis=0)

    with jax.named_scope("half"):
        picked = jnp.take(occ_coeff, batch_ids, axis=0)
        batch_coeff = lax.all_gather(picked, "occ", axis=1, tiled=True)
        left = batch_coeff.reshape(batch, atom_total, block_size)[:, blk_atoms[:, 0], :]
        left = left.reshape(batch, slots * block_size)
        offset = (blk_atoms[:, 1] - owner * step + atom_total) % atom_total
        offset = jnp.where(jnp.arange(slots, dtype=jnp.int32) < blk_count[0], offset, -1)
        offset = jnp.repeat(offset, block_size)
        hits = offset[None, :] == jnp.arange(window, dtype=jnp.int32)[:, None]
        spread = jnp.where(hits[:, None, :], left[None], jnp.bfloat16(0))
        mine = lax.dynamic_slice_in_dim(ints, rank * part, part, 3)
        half = jnp.einsum(
            "wik,knq->wniq",
            spread,
            mine.reshape(slots * block_size, block_size, part),
            preferred_element_type=jnp.float32,
        ).astype(jnp.bfloat16)
        half = half.reshape(depth, batch * part)
        along_z = [[z * ROWS + y for z in range(planes)] for y in range(ROWS)]
        half_all = lax.all_gather(half, "aux", axis=0, axis_index_groups=along_z)

    with jax.named_scope("fit"):
        source = jnp.arange(ranks * 2 * lane, dtype=jnp.int32)[:, None]
        target = jnp.arange(2 * ROWS * width, dtype=jnp.int32)[None, :]
        wanted = (
            (target // vir_group % ranks) * (2 * lane)
            + (target // (ROWS * width)) * lane
            + (target // width % ROWS) * vir_group
            + target % vir_group
        )
        place = (source == wanted).astype(jnp.bfloat16)
        fitted = pl.pallas_call(
            fit_kernel,
            grid=(planes // 2,),
            in_specs=[
                pl.BlockSpec((ranks, depth, 2 * lane), lambda s: (0, 0, s)),
                pl.BlockSpec((2, depth, batch * part), lambda s: (s, 0, 0)),
                pl.BlockSpec(place.shape, lambda s: (0, 0)),
            ],
            out_specs=pl.BlockSpec((ROWS, 2, width, batch * part), lambda s: (0, s, 0, 0)),
            out_shape=jax.ShapeDtypeStruct((ROWS, planes, width, batch * part), jnp.bfloat16),
        )(vir_all, half_all, place)
        along_y = [[z * ROWS + y for y in range(ROWS)] for z in range(planes)]
        regrouped = lax.all_to_all(
            fitted, "aux", split_axis=0, concat_axis=0, axis_index_groups=along_y, tiled=True
        )

    with jax.named_scope("gram"):
        total = batch * width
        kept = total // ranks
        partial = pl.pallas_call(
            gram_kernel,
            out_shape=jax.ShapeDtypeStruct((ranks, kept, total), jnp.bfloat16),
            in_specs=[pl.BlockSpec(memory_space=pltpu.VMEM)],
            out_specs=pl.BlockSpec(memory_space=pltpu.VMEM),
            scratch_shapes=[
                pltpu.VMEM((total, group_count * part), jnp.bfloat16),
                pltpu.VMEM((total, total), jnp.float32),
                pltpu.VMEM((kept, total), jnp.float32),
            ],
        )(regrouped.reshape(group_count, width, batch * part))
        shares = lax.all_to_all(partial, "occ", split_axis=0, concat_axis=0, tiled=True)
        pair_ints = jnp.sum(shares.astype(jnp.float32), axis=0)
        return pair_ints.reshape(batch, 1, vir_group, batch, width)


def solution(mesh):
    in_specs = (
        P(None, None, None, "aux"),
        P("aux", None),
        P("aux"),
        P(None, "occ"),
        P(None, "occ"),
        P(),
    )
    out_specs = P(None, "aux", "occ", None, None)
    return jax.shard_map(
        on_device, mesh=mesh, in_specs=in_specs, out_specs=out_specs, check_vma=False
    )
```

time: 455 us -> 175 us (0.38)
  the two profiles are of different devices: /device:TPU:8 before, /device:TPU:1 now
where the time goes in v1:
time: 175 us; the launch traced here: 174 us
  blocking collectives  80.5 us (46%)
  waiting for transfers between devices  40.3 us (23%)
  local copies, waits for them, and re-layouts  19.6 us (11%)
  between operations  14.2 us (8%)
  Pallas kernels  13.8 us (8%)
  other arithmetic  5.18 us (3%)
    all_gather x1, waiting for transfers between devices, on_device(): half_all = lax.all_gather(half, 'aux', axis=0, axis_index_groups=along_z)  39.8 us
    all_to_all x1, blocking collectives, on_device(): lax.all_to_all(fitted, 'aux', split_axis=0, concat_axis=0, axis_index_gro...  38.5 us
    all_to_all x1, blocking collectives, on_device(): lax.all_to_all(partial, 'occ', split_axis=0, concat_axis=0, tiled=True)  26.3 us
    all_gather x1, blocking collectives, on_device(): batch_coeff = lax.all_gather(picked, 'occ', axis=1, tiled=True)  15.8 us
    pallas_call x1, Pallas kernels, on_device(): pl.pallas_call(fit_kernel, grid=(planes // 2,), in_specs=[pl.BlockSpec((r...  7.87 us
    pallas_call x1, Pallas kernels, on_device(): pl.pallas_call(gram_kernel, out_shape=jax.ShapeDtypeStruct((ranks, kept,...  5.9 us
  transfers between devices with their start and end apart: 2, of which 2 were waited for; matrix products, arithmetic and copies ran while one was open for 9% of the time, Pallas kernels for 0%

profile of v1, /device:TPU:1, one launch (start us, length us, event | category | flops | bytes accessed | tf_op | source)
XLA Modules:
  0.0 174.1 jit_solution(4422094600091661206)
XLA Ops:
  6.5 0.0 copy-start
  6.5 0.0 all-gather.6.cloned.1.call-start
  6.5 1.9 %copy-done = bf16[4096,384]{1,0:T(8,128)(2,1)S(1)} copy-done((bf16[4096,384]{1,0:T(8,128)(2,1)S(1)}, bf16[4096,384]{1,0:T(8,128)(2,1)}, u32[]{:S(2)}) %copy-start) | copy-done | bytes 3145752
  8.4 0.4 constant_dynamic-slice_fusion.1
  8.8 1.2 pad.4
  10.0 0.0 copy-start.1
  10.0 0.0 copy-start.2
  10.0 3.0 %fusion.9 = bf16[3856,64]{1,0:T(8,128)(2,1)S(1)} fusion(s32[]{:T(128)S(6)} %select_n.105, bf16[4096,64]{1,0:T(8,128)(2,1)} %pad.4, bf16[144,64]{1,0:T(8,128)(2,1)S(1)} %pad_slice_fusion), kind=kLoop, calls=%fused_computation.11 | loop fusion | flops 987136 | bytes 1036292 | tf_op jit(solution)/shard_map/vir_rows/concatenate | solution.py:86
  13.0 0.7 fusion.37
  13.7 1.9 %concatenate.7 = bf16[272,512]{1,0:T(8,128)(2,1)} concatenate(bf16[272,64]{1,0:T(8,128)(2,1)} %get-tuple-element.12, bf16[272,64]{1,0:T(8,128)(2,1)} %get-tuple-element.11, bf16[272,64]{1,0:T(8,128)(2,1)} %get-tuple-element.10, bf16[272,64]{1,0:T(8,128)(2,1)S(1)} %get-tuple-element.9, bf16[272,64]{1,0:T(8,128)(2,1)S(1)} %get-tuple-element.8, ...), dimensions={1} | concatenate | bytes 557056 | tf_op jit(solution)/shard_map/vir_rows/concatenate | solution.py:88
  15.6 0.0 all-gather.6.cloned.1.call-update
  15.6 0.0 all-gather.4.cloned.1.call-start
  16.3 0.0 copy-done.1
  16.3 0.1 broadcast_in_dim.47
  16.4 0.1 eq.40
  16.5 0.0 copy-done.2
  16.5 2.1 %gather_fusion = bf16[8,512]{1,0:T(8,128)(2,1)S(1)} fusion(bf16[1280,512]{1,0:T(8,128)(2,1)} %param.9, s32[1024]{0:T(1024)S(1)} %pad_clamp_fusion.1), kind=kCustom, calls=%fused_computation | custom fusion | bytes 16416 | tf_op jit(solution)/shard_map/half/jit(_take)/gather | solution.py:94
  18.6 0.1 broadcast_select_fusion
  18.7 15.8 %all_gather.14 = bf16[8,4096]{1,0:T(8,128)(2,1)S(1)} all-gather(bf16[8,512]{1,0:T(8,128)(2,1)S(1)} %broadcast_select_fusion), channel_id=1, replica_groups=mesh['aux'=32,'occ'=8] {'occ'}, dimensions={1}, use_global_device_ids=true | all-gather | bytes 73728 | tf_op jit(solution)/shard_map/half/all_gather | solution.py:95
  34.5 1.2 reshape.162
  35.6 2.2 %copy.16 = bf16[8,256,16]{2,0,1:T(8,128)(2,1)} copy(bf16[8,256,16]{2,1,0:T(8,128)(2,1)} %reshape.162) | data formatting | bytes 131072 | tf_op jit(solution)/shard_map/half/reshape | solution.py:96
  37.8 1.6 gather_fusion.1
  39.5 0.1 broadcast_in_dim.52
  39.6 2.3 %constant_dynamic-slice_fusion = bf16[32,16,16,64]{3,2,1,0:T(8,128)(2,1)S(1)} fusion(bf16[32,16,16,512]{3,2,1,0:T(8,128)(2,1)} %param.6, s32[]{:T(128)S(6)} %select_n.106), kind=kLoop, calls=%fused_computation.63 | loop fusion | bytes 2097156 | tf_op jit(solution)/shard_map/half/dynamic_slice | solution.py:103
  41.9 0.6 fusion.6
  42.5 0.9 copy.19
  43.4 2.1 %reshape.163 = bf16[1,272,512]{2,1,0:T(8,128)(2,1)} reshape(bf16[17,16,8,64]{3,2,1,0:T(8,128)(2,1)} %copy.19) | data formatting | bytes 557056 | tf_op jit(solution)/shard_map/half/all_gather;half/reshape | solution.py:112
  45.5 0.0 all-gather.4.cloned.1.call-update
  45.6 1.9 %fusion.place_ref = bf16[1024,768]{1,0:T(8,128)(2,1)} fusion(s32[768]{0:T(1024)S(1)} %fusion.24), kind=kLoop, calls=%fused_computation.3 | loop fusion | flops 1572864 | bytes 1575936 | tf_op jit(solution)/shard_map/fit/convert_element_type | solution.py:123
  47.4 0.5 all-gather.6.cloned.1.call-done
  47.9 39.8 %all-gather.4.cloned.1.call-done.half_ref = bf16[8,272,512]{2,1,0:T(8,128)(2,1)} async-done(((bf16[1,272,512]{2,1,0:T(8,128)(2,1)}), bf16[8,272,512]{2,1,0:T(8,128)(2,1)}) %all-gather.4.cloned.1.call-update) | async-done | bytes 2228240 | tf_op jit(solution)/shard_map/half/all_gather | solution.py:112
  87.7 7.9 %fit.1 = bf16[4,8,96,512]{3,2,1,0:T(8,128)(2,1)} custom-call(bf16[8,272,512]{2,1,0:T(8,128)(2,1)} %bitcast.20, bf16[8,272,512]{2,1,0:T(8,128)(2,1)} %all-gather.4.cloned.1.call-done.half_ref, bf16[1024,768]{1,0:T(8,128)(2,1)} %fusion.place_ref), custom_call_target="tpu_custom_call" | custom-call | tf_op jit(solution)/shard_map/fit/pallas_call | solution.py:124
  95.6 38.5 %all_to_all.10 = bf16[4,8,96,512]{3,2,1,0:T(8,128)(2,1)} all-to-all(bf16[4,8,96,512]{3,2,1,0:T(8,128)(2,1)} %fit.1), channel_id=1, replica_groups={{0,8,16,24},{32,40,48,56},{64,72,80,88},{96,104,112,120},{128,136,144,1..., dimensions={0} | all-to-all | bytes 6291456 | tf_op jit(solution)/shard_map/fit/all_to_all | solution.py:136
  134.0 5.9 %gram.1 = bf16[8,96,768]{2,1,0:T(8,128)(2,1)} custom-call(bf16[32,96,512]{2,1,0:T(8,128)(2,1)} %bitcast.19), custom_call_target="tpu_custom_call" | custom-call | tf_op jit(solution)/shard_map/gram/pallas_call | solution.py:143
  139.9 26.3 %all_to_all.11 = bf16[8,96,768]{2,1,0:T(8,128)(2,1)S(1)} all-to-all(bf16[8,96,768]{2,1,0:T(8,128)(2,1)} %gram.1), channel_id=1, replica_groups=mesh['aux'=32,'occ'=8] {'occ'}, dimensions={0} | all-to-all | bytes 2359296 | tf_op jit(solution)/shard_map/gram/all_to_all | solution.py:154
  166.2 0.2 convert_reduce_fusion
  166.3 0.9 reshape.165
  (10 shorter events, 0.1 us)
Async XLA Ops:
  6.5 1.9 %copy-start = (bf16[4096,384]{1,0:T(8,128)(2,1)S(1)}, bf16[4096,384]{1,0:T(8,128)(2,1)}, u32[]{:S(2)}) copy-start(bf16[4096,384]{1,0:T(8,128)(2,1)} %param.10) | copy-start | bytes 9437188
  6.5 41.4 %all-gather.6.cloned.1.call-start = ((), (), s32[]{:S(2)}) async-start(), calls=%async_computation.3 | async-start | bytes 2506752 | tf_op jit(solution)/shard_map/vir_rows/all_gather | solution.py:91
  10.0 6.3 %copy-start.1 = (s32[32,2]{0,1:T(2,128)S(1)}, s32[32,2]{0,1:T(2,128)}, u32[]{:S(2)}) copy-start(s32[32,2]{0,1:T(2,128)} %param.7) | copy-start | bytes 772
  10.0 6.5 %copy-start.2 = (s32[8]{0:T(128)S(1)}, s32[8]{0:T(128)}, u32[]{:S(2)}) copy-start(s32[8]{0:T(128)} %param.11) | copy-start | bytes 100
  15.6 72.1 %all-gather.4.cloned.1.call-start = ((), (), s32[]{:S(2)}) async-start(), calls=%async_computation.2 | async-start | bytes 2506752 | tf_op jit(solution)/shard_map/half/all_gather | solution.py:112
Sparse Core Ops, SparseCore 0:
  15.7 32.1 all-gather.5
  49.7 37.9 all-gather.3

commit v2 on v1

v2 whole, which is shorter than its diff:
```python
import jax
import jax.numpy as jnp
from jax import lax
from jax.experimental import pallas as pl
from jax.experimental.pallas import tpu as pltpu
from jax.sharding import PartitionSpec as P

ROWS = 4


def exchange_kernel(
    vir_ref, half_ref, place_ref, out_ref,
    held, own, stage, relay, arrived, rows, gram, sorted_rows,
    ring_send, ring_recv, step_send, step_recv, pass_send, pass_recv,
):
    owner, rank = lax.axis_index("aux"), lax.axis_index("occ")
    plane, row = owner // ROWS, owner % ROWS
    blocks = own.shape[0]
    above, below = lax.rem(plane + 1, blocks) * ROWS + row, lax.rem(plane + blocks - 1, blocks) * ROWS + row
    after = plane * ROWS + lax.rem(row + 1, ROWS)
    before = plane * ROWS + lax.rem(row + ROWS - 1, ROWS)
    ranks = vir_ref.shape[0]
    width, lanes = own.shape[1], own.shape[2]
    batch = gram.shape[0] // width
    part = lanes // batch
    span = ROWS * width

    barrier = pltpu.get_barrier_semaphore()
    for peer in (above, below, after, before):
        pl.semaphore_signal(
            barrier, inc=1, device_id=(peer, rank), device_id_type=pl.DeviceIdType.MESH
        )
    pl.semaphore_wait(barrier, 4)

    def send(source, target, send_sem, recv_sem, peer):
        copy = pltpu.make_async_remote_copy(
            src_ref=source,
            dst_ref=target,
            send_sem=send_sem,
            recv_sem=recv_sem,
            device_id=(peer, rank),
            device_id_type=pl.DeviceIdType.MESH,
        )
        copy.start()
        return copy

    ring, direct, passed = {}, {}, {}

    def send_ring(b, source):
        ring[b] = send(
            source, held.at[b - 1], ring_send.at[b - 1], ring_recv.at[b - 1],
            above if b % 2 else below,
        )

    def pass_on(b):
        direct[b, 2].wait_recv()
        passed[b] = send(
            relay.at[b], arrived.at[1, b], pass_send.at[b], pass_recv.at[b],
            before if b % 2 else after,
        )

    def accumulate(p):
        first, second = 2 * p, 2 * p + 1
        for b in (first, second):
            direct[b, 1].wait_recv()
            direct[b, 3].wait_recv()
            passed[b].wait_recv()
        for r in range(ROWS):
            for h in range(batch // 2):
                cols = slice(2 * part * h, 2 * part * (h + 1))
                if r == 0:
                    one, two = own[first, :, cols], own[second, :, cols]
                else:
                    one, two = arrived[r - 1, first, :, cols], arrived[r - 1, second, :, cols]
                place = slice(2 * part * r, 2 * part * (r + 1))
                rows[width * 2 * h : width * (2 * h + 1), place] = jnp.concatenate(
                    [one[:, :part], two[:, :part]], axis=1
                )
                rows[width * (2 * h + 1) : width * (2 * h + 2), place] = jnp.concatenate(
                    [one[:, part:], two[:, part:]], axis=1
                )
        half = rows.shape[0] // 2
        for t in range(2):
            product = lax.dot_general(
                rows[half * t : half * (t + 1)],
                rows[...],
                (((1,), (1,)), ((), ())),
                preferred_element_type=jnp.float32,
            )
            if p == 0:
                gram[half * t : half * (t + 1)] = product
            else:
                gram[half * t : half * (t + 1)] += product

    send_ring(1, half_ref)
    send_ring(2, half_ref)
    for b in range(blocks):
        if b > 0:
            ring[b].wait_recv()
            if b + 2 < blocks:
                send_ring(b + 2, held.at[b - 1])
        if b % 2 == 0:
            wide = jnp.concatenate(
                [vir_ref[a, :, 64 * b : 64 * (b + 2)] for a in range(ranks)], axis=1
            )
            placed = jnp.dot(
                wide, place_ref[...], preferred_element_type=jnp.float32
            ).astype(jnp.bfloat16)
        t = b % 2
        summed = lax.dot_general(
            placed[:, span * t : span * (t + 1)],
            half_ref[...] if b == 0 else held[b - 1],
            (((0,), (0,)), ((), ())),
            preferred_element_type=jnp.float32,
        ).astype(jnp.bfloat16)
        own[b] = summed[:width]
        for r in range(1, ROWS):
            stage[b, r - 1] = summed[width * r : width * (r + 1)]
        direct[b, 1] = send(
            stage.at[b, 0], arrived.at[0, b], step_send.at[b, 0], step_recv.at[b, 0], after
        )
        direct[b, 3] = send(
            stage.at[b, 2], arrived.at[2, b], step_send.at[b, 2], step_recv.at[b, 2], before
        )
        direct[b, 2] = send(
            stage.at[b, 1], relay.at[b], step_send.at[b, 1], step_recv.at[b, 1],
            before if b % 2 else after,
        )
        if b > 0:
            pass_on(b - 1)
        if b % 2 and b > 2:
            accumulate((b - 3) // 2)
    pass_on(blocks - 1)
    accumulate(blocks // 2 - 1)
    for copy in [*ring.values(), *direct.values(), *passed.values()]:
        copy.wait_send()

    kept = width // ranks
    for a in range(ranks):
        for i in range(batch):
            sorted_rows[kept * i : kept * (i + 1)] = gram[
                width * i + kept * a : width * i + kept * (a + 1)
            ]
        out_ref[a] = sorted_rows[...].astype(jnp.bfloat16)


def ring_order(count):
    order = [0]
    for k in range(1, count // 2 + 1):
        order += [-k, k]
    return order[:count]


def on_device(ints, blk_atoms, blk_count, occ_coeff, vir_coeff, batch_ids):
    batch = batch_ids.shape[0]
    slots, block_size = ints.shape[0], ints.shape[1]
    aux_local = ints.shape[3]
    ranks = lax.axis_size("occ")
    group_count = lax.axis_size("aux")
    planes = group_count // ROWS
    owner, rank = lax.axis_index("aux"), lax.axis_index("occ")
    plane, row = owner // ROWS, owner % ROWS
    atom_total = vir_coeff.shape[0] // block_size
    step = atom_total // group_count
    window = 2 * step + 1
    depth = window * block_size
    part = aux_local // ranks
    vir_group = vir_coeff.shape[1] // group_count
    width = vir_group * ranks
    lane = 64

    with jax.named_scope("vir_rows"):
        cols = lax.dynamic_slice_in_dim(vir_coeff, plane * (ROWS * vir_group), ROWS * vir_group, 1)
        cols = jnp.pad(cols, ((0, 0), (0, lane - ROWS * vir_group)))
        cols = jnp.concatenate([cols, cols[:depth]], axis=0)
        pieces = []
        for shift in ring_order(planes):
            source = ((plane + shift + planes) % planes) * ROWS + row
            pieces.append(lax.dynamic_slice_in_dim(cols, source * (step * block_size), depth, 0))
        vir_rows = jnp.concatenate(pieces, axis=1)
        vir_all = lax.all_gather(vir_rows, "occ", axis=0)

    with jax.named_scope("half"):
        picked = jnp.take(occ_coeff, batch_ids, axis=0)
        batch_coeff = lax.all_gather(picked, "occ", axis=1, tiled=True)
        left = batch_coeff.reshape(batch, atom_total, block_size)[:, blk_atoms[:, 0], :]
        left = left.reshape(batch, slots * block_size)
        offset = (blk_atoms[:, 1] - owner * step + atom_total) % atom_total
        offset = jnp.where(jnp.arange(slots, dtype=jnp.int32) < blk_count[0], offset, -1)
        offset = jnp.repeat(offset, block_size)
        hits = offset[None, :] == jnp.arange(window, dtype=jnp.int32)[:, None]
        spread = jnp.where(hits[:, None, :], left[None], jnp.bfloat16(0))
        mine = lax.dynamic_slice_in_dim(ints, rank * part, part, 3)
        half = jnp.einsum(
            "wik,knq->wniq",
            spread,
            mine.reshape(slots * block_size, block_size, part),
            preferred_element_type=jnp.float32,
        ).astype(jnp.bfloat16)
        half = half.reshape(depth, batch * part)

    with jax.named_scope("fit"):
        source = jnp.arange(ranks * 2 * lane, dtype=jnp.int32)[:, None]
        target = jnp.arange(2 * ROWS * width, dtype=jnp.int32)[None, :]
        wanted = (
            (target // vir_group % ranks) * (2 * lane)
            + (target // (ROWS * width)) * lane
            + ((target // width + row) % ROWS) * vir_group
            + target % vir_group
        )
        place = (source == wanted).astype(jnp.bfloat16)
        total = batch * width
        kept = total // ranks
        piece = (width, batch * part)
        dma = pltpu.SemaphoreType.DMA
        partial = pl.pallas_call(
            exchange_kernel,
            out_shape=jax.ShapeDtypeStruct((ranks, kept, total), jnp.bfloat16),
            in_specs=[pl.BlockSpec(memory_space=pltpu.VMEM)] * 3,
            out_specs=pl.BlockSpec(memory_space=pltpu.VMEM),
            scratch_shapes=[
                pltpu.VMEM((planes - 1, depth, batch * part), jnp.bfloat16),
                pltpu.VMEM((planes, *piece), jnp.bfloat16),
                pltpu.VMEM((planes, ROWS - 1, *piece), jnp.bfloat16),
                pltpu.VMEM((planes, *piece), jnp.bfloat16),
                pltpu.VMEM((ROWS - 1, planes, *piece), jnp.bfloat16),
                pltpu.VMEM((total, ROWS * 2 * part), jnp.bfloat16),
                pltpu.VMEM((total, total), jnp.float32),
                pltpu.VMEM((kept, total), jnp.float32),
                dma((planes - 1,)),
                dma((planes - 1,)),
                dma((planes, ROWS - 1)),
                dma((planes, ROWS - 1)),
                dma((planes,)),
                dma((planes,)),
            ],
            compiler_params=pltpu.CompilerParams(collective_id=0, has_side_effects=True),
        )(vir_all, half, place)

    with jax.named_scope("pairs"):
        shares = lax.all_to_all(partial, "occ", split_axis=0, concat_axis=0, tiled=True)
        pair_ints = jnp.sum(shares.astype(jnp.float32), axis=0)
        return pair_ints.reshape(batch, 1, vir_group, batch, width)


def solution(mesh):
    in_specs = (
        P(None, None, None, "aux"),
        P("aux", None),
        P("aux"),
        P(None, "occ"),
        P(None, "occ"),
        P(),
    )
    out_specs = P(None, "aux", "occ", None, None)
    return jax.shard_map(
        on_device, mesh=mesh, in_specs=in_specs, out_specs=out_specs, check_vma=False
    )
```

time: 175 us -> 131 us (0.75)
  blocking collectives: 80.5 us -> 39.8 us
  waiting for transfers between devices: 40.3 us -> 0.34 us
  Pallas kernels: 13.8 us -> 50.3 us
    all_gather x1 -> x0, waiting for transfers between devices: 39.8 us -> none  [on_device(): half_all = lax.all_gather(half, 'aux', axis=0, axis_index_groups=along_z)]
    all_to_all x1 -> x0, blocking collectives: 38.5 us -> none  [on_device(): lax.all_to_all(fitted, 'aux', split_axis=0, concat_axis=0, axis_index_gro...]
    pallas_call x2 -> x1, Pallas kernels: 13.8 us -> 50.3 us  [on_device(): pl.pallas_call(exchange_kernel, out_shape=jax.ShapeDtypeStruct((ranks, ke...]
    all_to_all x1, blocking collectives: 26.3 us -> 23.8 us  [on_device(): lax.all_to_all(partial, 'occ', split_axis=0, concat_axis=0, tiled=True)]
  transfers between devices with their start and end apart: 2 -> 1, of which waited for: 2 -> 1; matrix products, arithmetic and copies ran while one was open for 9% -> 12% of each run, Pallas kernels for 0% -> 0%
where the time goes in v2:
time: 131 us; the launch traced here: 130 us
  Pallas kernels  50.3 us (38%)
  blocking collectives  39.8 us (30%)
  local copies, waits for them, and re-layouts  19.1 us (15%)
  between operations  14.2 us (11%)
  other arithmetic  5.56 us (4%)
    pallas_call x1, Pallas kernels, on_device(): pl.pallas_call(exchange_kernel, out_shape=jax.ShapeDtypeStruct((ranks, ke...  50.3 us
    all_to_all x1, blocking collectives, on_device(): lax.all_to_all(partial, 'occ', split_axis=0, concat_axis=0, tiled=True)  23.8 us
    all_gather x1, blocking collectives, on_device(): batch_coeff = lax.all_gather(picked, 'occ', axis=1, tiled=True)  16 us
    concatenate x2, other arithmetic, on_device(): cols = jnp.concatenate([cols, cols[:depth]], axis=0)  3.45 us
    reshape x2, local copies, waits for them, and re-layouts, on_device(): batch_coeff.reshape(batch, atom_total, block_size)[:, blk_atoms[:, 0], :]  3.38 us
  transfers between devices with their start and end apart: 1, of which 1 were waited for; matrix products, arithmetic and copies ran while one was open for 12% of the time, Pallas kernels for 0%

profile of v2, /device:TPU:1, one launch (start us, length us, event | category | flops | bytes accessed | tf_op | source)
XLA Modules:
  0.0 129.7 jit_solution(15597970211798549334)
XLA Ops:
  6.5 0.0 copy-start
  6.5 0.0 all-gather.3.cloned.1.call-start
  6.5 1.9 %copy-done = bf16[4096,384]{1,0:T(8,128)(2,1)S(1)} copy-done((bf16[4096,384]{1,0:T(8,128)(2,1)S(1)}, bf16[4096,384]{1,0:T(8,128)(2,1)}, u32[]{:S(2)}) %copy-start) | copy-done | bytes 3145752
  8.4 0.4 constant_dynamic-slice_fusion.1
  8.8 1.2 pad.4
  10.0 0.0 copy-start.1
  10.0 1.3 fusion.21
  11.3 0.0 copy-done.1
  11.3 0.0 copy-start.2
  11.3 0.0 copy-start.3
  11.3 2.2 %fusion.14 = (bf16[272,64]{1,0:T(8,128)(2,1)S(1)}, bf16[272,64]{1,0:T(8,128)(2,1)S(1)}, bf16[272,64]{1,0:T(8,128)(2,1)}, bf16[272,64]{1,0:T(8,128)(2,1)}, bf16[272,64]{1,0:T(8,128)(2,1)}, /*index=5*/bf16[272,64]{1,0:T(8,128)(2,1)}) fusion(s32[]{:T(128)S(6)} %select_n.173, bf16[4096,64]{1,0:T(8,128)(2,1)S(1)} %copy-done.1, ...), kind=kLoop, calls=%fused_computation.30 | loop fusion | flops 417792 | bytes 768024 | tf_op jit(solution)/shard_map/vir_rows/concatenate | solution.py:175
  13.5 1.9 %concatenate.7 = bf16[272,512]{1,0:T(8,128)(2,1)} concatenate(bf16[272,64]{1,0:T(8,128)(2,1)S(1)} %get-tuple-element.6, bf16[272,64]{1,0:T(8,128)(2,1)} %get-tuple-element.7, bf16[272,64]{1,0:T(8,128)(2,1)} %get-tuple-element.8, bf16[272,64]{1,0:T(8,128)(2,1)} %get-tuple-element.9, bf16[272,64]{1,0:T(8,128)(2,1)} %get-tuple-element.10, bf16[272,64]{1,0:T(8,128)(2,1)S(1)} %get-tuple-element.12, ...), dimensions={1} | concatenate | bytes 557056 | tf_op jit(solution)/shard_map/vir_rows/concatenate | solution.py:180
  15.4 0.0 all-gather.3.cloned.1.call-update
  16.1 0.0 copy-done.2
  16.1 0.1 broadcast_in_dim.47
  16.2 0.1 eq.48
  16.3 0.0 copy-done.3
  16.3 2.1 %gather_fusion = bf16[8,512]{1,0:T(8,128)(2,1)S(1)} fusion(bf16[1280,512]{1,0:T(8,128)(2,1)} %param.9, s32[1024]{0:T(1024)S(1)} %pad_clamp_fusion.1), kind=kCustom, calls=%fused_computation | custom fusion | bytes 16416 | tf_op jit(solution)/shard_map/half/jit(_take)/gather | solution.py:184
  18.4 0.1 broadcast_select_fusion
  18.4 16.0 %all_gather.11 = bf16[8,4096]{1,0:T(8,128)(2,1)S(1)} all-gather(bf16[8,512]{1,0:T(8,128)(2,1)S(1)} %broadcast_select_fusion), channel_id=1, replica_groups=mesh['aux'=32,'occ'=8] {'occ'}, dimensions={1}, use_global_device_ids=true | all-gather | bytes 73728 | tf_op jit(solution)/shard_map/half/all_gather | solution.py:185
  34.4 1.2 reshape.161
  35.6 2.2 %copy.9 = bf16[8,256,16]{2,0,1:T(8,128)(2,1)} copy(bf16[8,256,16]{2,1,0:T(8,128)(2,1)} %reshape.161) | data formatting | bytes 131072 | tf_op jit(solution)/shard_map/half/reshape | solution.py:186
  37.8 1.6 %gather_fusion.1 = bf16[32,8,16]{2,1,0:T(8,128)(2,1)S(1)} fusion(bf16[8,256,16]{2,0,1:T(8,128)(2,1)} %copy.9, s32[1024]{0:T(1024)S(1)} %pad_clamp_fusion), kind=kCustom, calls=%fused_computation.1 | custom fusion | bytes 16512 | tf_op jit(solution)/shard_map/half/gather | solution.py:186
  39.4 0.1 broadcast_in_dim.52
  39.6 2.3 %constant_dynamic-slice_fusion = bf16[32,16,16,64]{3,2,1,0:T(8,128)(2,1)S(1)} fusion(bf16[32,16,16,512]{3,2,1,0:T(8,128)(2,1)} %param.6, s32[]{:T(128)S(6)} %select_n.174), kind=kLoop, calls=%fused_computation.60 | loop fusion | bytes 2097156 | tf_op jit(solution)/shard_map/half/dynamic_slice | solution.py:193
  41.9 0.6 fusion.6
  42.5 0.9 copy.12
  43.4 2.1 %reshape.162.half_ref = bf16[272,512]{1,0:T(8,128)(2,1)} reshape(bf16[17,16,8,64]{3,2,1,0:T(8,128)(2,1)} %copy.12) | data formatting | bytes 557056 | tf_op jit(solution)/shard_map/half/reshape | solution.py:200
  45.6 1.8 %fusion.place_ref = bf16[1024,768]{1,0:T(8,128)(2,1)} fusion(s32[768]{0:T(1024)S(1)} %fusion.32), kind=kLoop, calls=%fused_computation.11 | loop fusion | flops 1572864 | bytes 1575936 | tf_op jit(solution)/shard_map/fit/convert_element_type | solution.py:211
  47.4 0.3 all-gather.3.cloned.1.call-done
  47.7 50.3 %fit.1 = bf16[8,96,768]{2,1,0:T(8,128)(2,1)} custom-call(bf16[8,272,512]{2,1,0:T(8,128)(2,1)} %bitcast.18, bf16[272,512]{1,0:T(8,128)(2,1)} %reshape.162.half_ref, bf16[1024,768]{1,0:T(8,128)(2,1)} %fusion.place_ref), custom_call_target="tpu_custom_call" | custom-call | tf_op jit(solution)/shard_map/fit/pallas_call | solution.py:216
  98.0 23.8 %all_to_all.5 = bf16[8,96,768]{2,1,0:T(8,128)(2,1)S(1)} all-to-all(bf16[8,96,768]{2,1,0:T(8,128)(2,1)} %fit.1), channel_id=1, replica_groups=mesh['aux'=32,'occ'=8] {'occ'}, dimensions={0} | all-to-all | bytes 2359296 | tf_op jit(solution)/shard_map/pairs/all_to_all | solution.py:241
  121.8 0.2 convert_reduce_fusion
  121.9 0.9 reshape.163
  (10 shorter events, 0.1 us)
Async XLA Ops:
  6.5 1.9 %copy-start = (bf16[4096,384]{1,0:T(8,128)(2,1)S(1)}, bf16[4096,384]{1,0:T(8,128)(2,1)}, u32[]{:S(2)}) copy-start(bf16[4096,384]{1,0:T(8,128)(2,1)} %param.10) | copy-start | bytes 9437188
  6.5 41.2 %all-gather.3.cloned.1.call-start = ((), (), s32[]{:S(2)}) async-start(), calls=%async_computation.1 | async-start | bytes 2506752 | tf_op jit(solution)/shard_map/vir_rows/all_gather | solution.py:181
  10.0 1.3 copy-start.1
  11.3 4.8 %copy-start.2 = (s32[32,2]{0,1:T(2,128)S(1)}, s32[32,2]{0,1:T(2,128)}, u32[]{:S(2)}) copy-start(s32[32,2]{0,1:T(2,128)} %param.7) | copy-start | bytes 772
  11.3 4.9 %copy-start.3 = (s32[8]{0:T(128)S(1)}, s32[8]{0:T(128)}, u32[]{:S(2)}) copy-start(s32[8]{0:T(128)} %param.11) | copy-start | bytes 100
Sparse Core Ops, SparseCore 0:
  15.5 32.1 all-gather.2

commit v3 on v2

--- a/solution.py
+++ b/solution.py
@@ -10,8 +10,10 @@
 
 def exchange_kernel(
     vir_ref, half_ref, place_ref, out_ref,
-    held, own, stage, relay, arrived, rows, gram, sorted_rows,
-    ring_send, ring_recv, step_send, step_recv, pass_send, pass_recv,
+    vir_held, held, own, stage, relay, arrived, rows, gram, sorted_rows,
+    joined, mine, others,
+    vir_send, vir_recv, ring_send, ring_recv, step_send, step_recv, pass_send, pass_recv,
+    join_send, join_recv, sum_send, sum_recv,
 ):
     owner, rank = lax.axis_index("aux"), lax.axis_index("occ")
     plane, row = owner // ROWS, owner % ROWS
@@ -19,32 +21,46 @@
     above, below = lax.rem(plane + 1, blocks) * ROWS + row, lax.rem(plane + blocks - 1, blocks) * ROWS + row
     after = plane * ROWS + lax.rem(row + 1, ROWS)
     before = plane * ROWS + lax.rem(row + ROWS - 1, ROWS)
-    ranks = vir_ref.shape[0]
+    parts, ranks = vir_ref.shape[0], vir_held.shape[1] + 1
+    chips = ranks // 2
+    core = lax.rem(rank, 2)
+    partner = rank + 1 - 2 * core
     width, lanes = own.shape[1], own.shape[2]
     batch = gram.shape[0] // width
     part = lanes // batch
     span = ROWS * width
 
     barrier = pltpu.get_barrier_semaphore()
-    for peer in (above, below, after, before):
-        pl.semaphore_signal(
-            barrier, inc=1, device_id=(peer, rank), device_id_type=pl.DeviceIdType.MESH
-        )
-    pl.semaphore_wait(barrier, 4)
-
-    def send(source, target, send_sem, recv_sem, peer):
+    near = [(peer, rank) for peer in (above, below, after, before)]
+    near += [(owner, partner)] + [(owner, lax.rem(rank + 2 * k, ranks)) for k in range(1, chips)]
+    for peer in near:
+        pl.semaphore_signal(barrier, inc=1, device_id=peer, device_id_type=pl.DeviceIdType.MESH)
+    pl.semaphore_wait(barrier, len(near))
+
+    def send(source, target, send_sem, recv_sem, peer, peer_rank=rank):
         copy = pltpu.make_async_remote_copy(
             src_ref=source,
             dst_ref=target,
             send_sem=send_sem,
             recv_sem=recv_sem,
-            device_id=(peer, rank),
+            device_id=(peer, peer_rank),
             device_id_type=pl.DeviceIdType.MESH,
         )
         copy.start()
         return copy
 
-    ring, direct, passed = {}, {}, {}
+    ring, direct, passed, spread, joins, sums = {}, {}, {}, {}, {}, {}
+
+    def send_vir(p, k, d, source, peer_rank):
+        j = 2 * k + d - 1
+        spread[p, j] = send(
+            source, vir_held.at[p, j], vir_send.at[p, j], vir_recv.at[p, j], owner, peer_rank
+        )
+
+    def pass_vir(p):
+        for k in range(1, chips):
+            spread[p, 2 * k - 1].wait_recv()
+            send_vir(p, k, 1, vir_held.at[p, 2 * k - 1], partner)
 
     def send_ring(b, source):
         ring[b] = send(
@@ -94,14 +110,22 @@
 
     send_ring(1, half_ref)
     send_ring(2, half_ref)
+    for p in range(parts):
+        for k in range(1, chips):
+            send_vir(p, k, 0, vir_ref.at[p], lax.rem(rank + 2 * k, ranks))
+        send_vir(p, 0, 1, vir_ref.at[p], partner)
+    pass_vir(0)
     for b in range(blocks):
         if b > 0:
             ring[b].wait_recv()
             if b + 2 < blocks:
                 send_ring(b + 2, held.at[b - 1])
         if b % 2 == 0:
+            p = b // 2
+            for k in range(chips):
+                spread[p, 2 * k].wait_recv()
             wide = jnp.concatenate(
-                [vir_ref[a, :, 64 * b : 64 * (b + 2)] for a in range(ranks)], axis=1
+                [vir_ref[p]] + [vir_held[p, j] for j in range(ranks - 1)], axis=1
             )
             placed = jnp.dot(
                 wide, place_ref[...], preferred_element_type=jnp.float32
@@ -128,20 +152,79 @@
         )
         if b > 0:
             pass_on(b - 1)
+        if b % 2 and (b + 1) // 2 < parts:
+            pass_vir((b + 1) // 2)
         if b % 2 and b > 2:
             accumulate((b - 3) // 2)
     pass_on(blocks - 1)
     accumulate(blocks // 2 - 1)
-    for copy in [*ring.values(), *direct.values(), *passed.values()]:
-        copy.wait_send()
 
     kept = width // ranks
     for a in range(ranks):
         for i in range(batch):
-            sorted_rows[kept * i : kept * (i + 1)] = gram[
+            sorted_rows[a, kept * i : kept * (i + 1)] = gram[
                 width * i + kept * a : width * i + kept * (a + 1)
             ]
-        out_ref[a] = sorted_rows[...].astype(jnp.bfloat16)
+    chip = rank // 2
+    order = [*range(1, chips), 0]
+    for k in order:
+        theirs = 2 * lax.rem(chip + k, chips) + 1 - core
+        joins[k] = send(
+            sorted_rows.at[theirs], joined.at[k], join_send.at[k], join_recv.at[k], owner, partner
+        )
+    for k in order:
+        joins[k].wait_recv()
+        both = sorted_rows[2 * lax.rem(chip + k, chips) + core] + joined[k]
+        if k > 0:
+            mine[k - 1] = both.astype(jnp.bfloat16)
+            sums[k] = send(
+                mine.at[k - 1], others.at[k - 1], sum_send.at[k - 1], sum_recv.at[k - 1],
+                owner, lax.rem(rank + 2 * k, ranks),
+            )
+    for k in range(1, chips):
+        sums[k].wait_recv()
+        both += others[k - 1].astype(jnp.float32)
+    out_ref[...] = both
+    for group in (spread, ring, direct, passed, joins, sums):
+        for copy in group.values():
+            copy.wait_send()
+
+
+def pick_kernel(mine_ref, index_ref, left_ref, held, send_sem, recv_sem):
+    owner, rank = lax.axis_index("aux"), lax.axis_index("occ")
+    ranks = held.shape[0]
+    barrier = pltpu.get_barrier_semaphore()
+    peers = [(owner, lax.rem(rank + r, ranks)) for r in range(1, ranks)]
+    for peer in peers:
+        pl.semaphore_signal(barrier, inc=1, device_id=peer, device_id_type=pl.DeviceIdType.MESH)
+    pl.semaphore_wait(barrier, ranks - 1)
+    copies = []
+    for r in range(1, ranks):
+        copy = pltpu.make_async_remote_copy(
+            src_ref=mine_ref,
+            dst_ref=held.at[r],
+            send_sem=send_sem.at[r],
+            recv_sem=recv_sem.at[r],
+            device_id=peers[r - 1],
+            device_id_type=pl.DeviceIdType.MESH,
+        )
+        copy.start()
+        copies.append(copy)
+    span = mine_ref.shape[1]
+    column = lax.broadcasted_iota(jnp.int32, (span, index_ref.shape[1]), 0)
+    total = None
+    for r in range(ranks):
+        if r > 0:
+            copies[r - 1].wait_recv()
+        first = lax.rem(rank + ranks - r, ranks) * span
+        hits = jnp.where(column == index_ref[...] - first, 1.0, 0.0).astype(jnp.bfloat16)
+        term = jnp.dot(
+            mine_ref[...] if r == 0 else held[r], hits, preferred_element_type=jnp.float32
+        )
+        total = term if total is None else total + term
+    left_ref[...] = total.astype(jnp.bfloat16)
+    for copy in copies:
+        copy.wait_send()
 
 
 def ring_order(count):
@@ -149,6 +232,11 @@
     for k in range(1, count // 2 + 1):
         order += [-k, k]
     return order[:count]
+
+
+def slot_of(source, rank, ranks):
+    chips = ranks // 2
+    return 2 * ((rank // 2 - source // 2 + chips) % chips) + (source + rank) % 2
 
 
 def on_device(ints, blk_atoms, blk_count, occ_coeff, vir_coeff, batch_ids):
@@ -177,14 +265,27 @@
         for shift in ring_order(planes):
             source = ((plane + shift + planes) % planes) * ROWS + row
             pieces.append(lax.dynamic_slice_in_dim(cols, source * (step * block_size), depth, 0))
-        vir_rows = jnp.concatenate(pieces, axis=1)
-        vir_all = lax.all_gather(vir_rows, "occ", axis=0)
+        vir_rows = jnp.stack(
+            [jnp.concatenate(pieces[b : b + 2], axis=1) for b in range(0, planes, 2)]
+        )
 
     with jax.named_scope("half"):
         picked = jnp.take(occ_coeff, batch_ids, axis=0)
-        batch_coeff = lax.all_gather(picked, "occ", axis=1, tiled=True)
-        left = batch_coeff.reshape(batch, atom_total, block_size)[:, blk_atoms[:, 0], :]
-        left = left.reshape(batch, slots * block_size)
+        index = blk_atoms[:, 0, None] * block_size + jnp.arange(block_size, dtype=jnp.int32)
+        vmem = pl.BlockSpec(memory_space=pltpu.VMEM)
+        dma = pltpu.SemaphoreType.DMA
+        left = pl.pallas_call(
+            pick_kernel,
+            out_shape=jax.ShapeDtypeStruct((batch, slots * block_size), jnp.bfloat16),
+            in_specs=[vmem] * 2,
+            out_specs=vmem,
+            scratch_shapes=[
+                pltpu.VMEM((ranks, *picked.shape), jnp.bfloat16),
+                dma((ranks,)),
+                dma((ranks,)),
+            ],
+            compiler_params=pltpu.CompilerParams(collective_id=1, has_side_effects=True),
+        )(picked, index.reshape(1, slots * block_size))
         offset = (blk_atoms[:, 1] - owner * step + atom_total) % atom_total
         offset = jnp.where(jnp.arange(slots, dtype=jnp.int32) < blk_count[0], offset, -1)
         offset = jnp.repeat(offset, block_size)
@@ -203,7 +304,7 @@
         source = jnp.arange(ranks * 2 * lane, dtype=jnp.int32)[:, None]
         target = jnp.arange(2 * ROWS * width, dtype=jnp.int32)[None, :]
         wanted = (
-            (target // vir_group % ranks) * (2 * lane)
+            slot_of(target // vir_group % ranks, rank, ranks) * (2 * lane)
             + (target // (ROWS * width)) * lane
             + ((target // width + row) % ROWS) * vir_group
             + target % vir_group
@@ -212,13 +313,14 @@
         total = batch * width
         kept = total // ranks
         piece = (width, batch * part)
-        dma = pltpu.SemaphoreType.DMA
-        partial = pl.pallas_call(
+        chips = ranks // 2
+        pair_ints = pl.pallas_call(
             exchange_kernel,
-            out_shape=jax.ShapeDtypeStruct((ranks, kept, total), jnp.bfloat16),
-            in_specs=[pl.BlockSpec(memory_space=pltpu.VMEM)] * 3,
-            out_specs=pl.BlockSpec(memory_space=pltpu.VMEM),
+            out_shape=jax.ShapeDtypeStruct((kept, total), jnp.float32),
+            in_specs=[vmem] * 3,
+            out_specs=vmem,
             scratch_shapes=[
+                pltpu.VMEM((planes // 2, ranks - 1, depth, 2 * lane), jnp.bfloat16),
                 pltpu.VMEM((planes - 1, depth, batch * part), jnp.bfloat16),
                 pltpu.VMEM((planes, *piece), jnp.bfloat16),
                 pltpu.VMEM((planes, ROWS - 1, *piece), jnp.bfloat16),
@@ -226,20 +328,25 @@
                 pltpu.VMEM((ROWS - 1, planes, *piece), jnp.bfloat16),
                 pltpu.VMEM((total, ROWS * 2 * part), jnp.bfloat16),
                 pltpu.VMEM((total, total), jnp.float32),
-                pltpu.VMEM((kept, total), jnp.float32),
+                pltpu.VMEM((ranks, kept, total), jnp.float32),
+                pltpu.VMEM((chips, kept, total), jnp.float32),
+                pltpu.VMEM((chips - 1, kept, total), jnp.bfloat16),
+                pltpu.VMEM((chips - 1, kept, total), jnp.bfloat16),
+                dma((planes // 2, ranks - 1)),
+                dma((planes // 2, ranks - 1)),
                 dma((planes - 1,)),
                 dma((planes - 1,)),
                 dma((planes, ROWS - 1)),
                 dma((planes, ROWS - 1)),
                 dma((planes,)),
                 dma((planes,)),
+                dma((chips,)),
+                dma((chips,)),
+                dma((chips - 1,)),
+                dma((chips - 1,)),
             ],
             compiler_params=pltpu.CompilerParams(collective_id=0, has_side_effects=True),
-        )(vir_all, half, place)
-
-    with jax.named_scope("pairs"):
-        shares = lax.all_to_all(partial, "occ", split_axis=0, concat_axis=0, tiled=True)
-        pair_ints = jnp.sum(shares.astype(jnp.float32), axis=0)
+        )(vir_rows, half, place)
         return pair_ints.reshape(batch, 1, vir_group, batch, width)
 
 

time: 131 us -> 107 us (0.82)
  blocking collectives: 39.8 us -> 0 us
  Pallas kernels: 50.3 us -> 79.4 us
  between operations: 14.2 us -> 0.88 us
  local copies, waits for them, and re-layouts: 19.1 us -> 14.9 us
  other arithmetic: 5.56 us -> 8.23 us
  matrix products: 0.58 us -> 2.18 us
    pallas_call x1 -> x2, Pallas kernels: 50.3 us -> 79.4 us  [the longest x1 69.4 us: on_device(): pl.pallas_call(exchange_kernel, out_shape=jax.ShapeDtypeStruct((kept, tot...]
    all_to_all x1 -> x0, blocking collectives: 23.8 us -> none  [on_device(): lax.all_to_all(partial, 'occ', split_axis=0, concat_axis=0, tiled=True)]
    all_gather x1 -> x0, blocking collectives: 16 us -> none  [on_device(): batch_coeff = lax.all_gather(picked, 'occ', axis=1, tiled=True)]
    reshape x2 -> x0, local copies, waits for them, and re-layouts: 3.38 us -> none  [on_device(): batch_coeff.reshape(batch, atom_total, block_size)[:, blk_atoms[:, 0], :]]
    another operation x0 -> x3, other arithmetic: none -> 1.89 us  [on_device(): jnp.stack([jnp.concatenate(pieces[b:b + 2], axis=1) for b in range(0, pla...]
    concatenate x1 -> x0, local copies, waits for them, and re-layouts: 1.89 us -> none  [on_device(): vir_rows = jnp.concatenate(pieces, axis=1)]
    gather x2 -> x0, local copies, waits for them, and re-layouts: 1.65 us -> none  [on_device(): batch_coeff.reshape(batch, atom_total, block_size)[:, blk_atoms[:, 0], :]]
    dot_general x1, matrix products: 0.58 us -> 2.18 us  [on_device(): jnp.einsum('wik,knq->wniq', spread, mine.reshape(slots * block_size, bloc...]
  transfers between devices with their start and end apart: 1 -> 0, of which waited for: 1 -> 0; matrix products, arithmetic and copies ran while one was open for 12% -> 0% of each run, Pallas kernels for 0% -> 0%
where the time goes in v3:
time: 107 us; the launch traced here: 106 us
  Pallas kernels  79.4 us (74%)
  local copies, waits for them, and re-layouts  14.9 us (14%)
  other arithmetic  8.23 us (8%)
  matrix products  2.18 us (2%)
    pallas_call x1, Pallas kernels, on_device(): pl.pallas_call(exchange_kernel, out_shape=jax.ShapeDtypeStruct((kept, tot...  69.4 us
    pallas_call x1, Pallas kernels, on_device(): pl.pallas_call(pick_kernel, out_shape=jax.ShapeDtypeStruct((batch, slots...  9.97 us
    concatenate x2, other arithmetic, on_device(): cols = jnp.concatenate([cols, cols[:depth]], axis=0)  3.72 us
    dynamic_slice x1, local copies, waits for them, and re-layouts, on_device(): mine = lax.dynamic_slice_in_dim(ints, rank * part, part, 3)  3.63 us
    dot_general x1, matrix products, on_device(): jnp.einsum('wik,knq->wniq', spread, mine.reshape(slots * block_size, bloc...  2.18 us

profile of v3, /device:TPU:1, one launch (start us, length us, event | category | flops | bytes accessed | tf_op | source)
XLA Modules:
  0.0 105.6 jit_solution(5075319648763080111)
XLA Ops:
  0.0 0.0 copy-start
  0.0 1.9 %copy-done = bf16[4096,384]{1,0:T(8,128)(2,1)S(1)} copy-done((bf16[4096,384]{1,0:T(8,128)(2,1)S(1)}, bf16[4096,384]{1,0:T(8,128)(2,1)}, u32[]{:S(2)}) %copy-start) | copy-done | bytes 3145752
  1.9 0.4 constant_dynamic-slice_fusion.1
  2.3 1.2 %pad.4 = bf16[4096,64]{1,0:T(8,128)(2,1)} pad(bf16[4096,48]{1,0:T(8,128)(2,1)S(1)} %constant_dynamic-slice_fusion.1, bf16[]{:T(256)} %constant.188.clone.1), padding=0_0x0_16 | pad | bytes 917506 | tf_op jit(solution)/shard_map/vir_rows/jit(_pad)/pad | solution.py:262
  3.6 2.5 %fusion.15 = (bf16[272,64]{1,0:T(8,128)(2,1)S(1)}, bf16[272,64]{1,0:T(8,128)(2,1)S(1)}, bf16[272,64]{1,0:T(8,128)(2,1)S(1)}, bf16[272,64]{1,0:T(8,128)(2,1)S(1)}...) fusion(s32[]{:T(128)S(6)} %select_n.188, bf16[4096,64]{1,0:T(8,128)(2,1)} %pad.4, ...), kind=kLoop, calls=%fused_computation.30 | loop fusion | flops 417792 | bytes 768024 | tf_op jit(solution)/shard_map/vir_rows/concatenate | solution.py:263
  6.1 1.2 %fusion.21 = (bf16[272,64]{1,0:T(8,128)(2,1)S(1)}, bf16[272,64]{1,0:T(8,128)(2,1)S(1)}) fusion(s32[]{:T(128)S(6)} %select_n.200, bf16[4096,64]{1,0:T(8,128)(2,1)} %pad.4, bf16[272,64]{1,0:T(8,128)(2,1)S(1)} %pad_slice_fusion, s32[]{:T(128)S(6)} %select_n.202), kind=kLoop, calls=%fused_computation.36 | loop fusion | flops 139264 | bytes 628744 | tf_op jit(solution)/shard_map/vir_rows/concatenate | solution.py:263
  7.3 1.0 maximum_bitcast_fusion.2
  8.4 0.1 maximum_bitcast_fusion
  8.5 0.7 pad_maximum_fusion.vir_ref
  9.2 0.0 copy-start.1
  9.2 0.0 copy-start.2
  9.2 3.6 %constant_dynamic-slice_fusion = bf16[32,16,16,64]{3,2,1,0:T(8,128)(2,1)} fusion(bf16[32,16,16,512]{3,2,1,0:T(8,128)(2,1)} %param.6, s32[]{:T(128)S(6)} %select_n.203), kind=kLoop, calls=%fused_computation.74 | loop fusion | bytes 2097156 | tf_op jit(solution)/shard_map/half/dynamic_slice | solution.py:294
  13.5 0.0 copy-done.1
  13.6 0.1 broadcast_in_dim.46
  13.6 0.1 eq.50
  13.7 0.0 copy-done.2
  13.8 2.1 %gather_fusion = bf16[8,512]{1,0:T(8,128)(2,1)S(1)} fusion(bf16[1280,512]{1,0:T(8,128)(2,1)} %param.9, s32[1024]{0:T(1024)S(1)} %pad_clamp_fusion), kind=kCustom, calls=%fused_computation | custom fusion | bytes 16416 | tf_op jit(solution)/shard_map/half/jit(_take)/gather | solution.py:273
  15.8 0.7 broadcast_select_fusion.mine_ref
  16.5 0.1 iota_add_fusion
  16.6 0.7 add.360.index_ref
  17.2 10.0 %half.1 = bf16[8,512]{1,0:T(8,128)(2,1)} custom-call(bf16[8,512]{1,0:T(8,128)(2,1)} %broadcast_select_fusion.mine_ref, s32[1,512]{1,0:T(1,128)} %add.360.index_ref), custom_call_target="tpu_custom_call" | custom-call | tf_op jit(solution)/shard_map/half/pallas_call | solution.py:277
  27.2 2.2 %fusion.6 = bf16[17,16,8,64]{3,0,2,1:T(8,128)(2,1)S(1)} fusion(bf16[512,16,64,1]{2,1,0,3:T(8,128)(2,1)} %bitcast.25, pred[17,512]{1,0:T(8,128)(4,1)S(1)} %iota_compare_fusion.1, bf16[8,512]{1,0:T(8,128)(2,1)} %half.1), kind=kOutput, calls=%fused_computation.14 | convolution fusion | flops 142815232 | bytes 1344000 | tf_op jit(solution)/shard_map/half/wik,knq->wniq/dot_general | solution.py:295
  29.4 0.9 copy.11
  30.3 2.1 %reshape.257.half_ref = bf16[272,512]{1,0:T(8,128)(2,1)} reshape(bf16[17,16,8,64]{3,2,1,0:T(8,128)(2,1)} %copy.11) | data formatting | bytes 557056 | tf_op jit(solution)/shard_map/half/reshape | solution.py:301
  32.5 1.8 %fusion.place_ref = bf16[1024,768]{1,0:T(8,128)(2,1)} fusion(s32[768]{0:T(1024)S(1)} %fusion.32), kind=kLoop, calls=%fused_computation.10 | loop fusion | flops 1572864 | bytes 1575936 | tf_op jit(solution)/shard_map/fit/convert_element_type | solution.py:312
  34.3 69.4 %fit.1 = f32[96,768]{1,0:T(8,128)} custom-call(bf16[4,272,128]{2,1,0:T(8,128)(2,1)} %pad_maximum_fusion.vir_ref, bf16[272,512]{1,0:T(8,128)(2,1)} %reshape.257.half_ref, bf16[1024,768]{1,0:T(8,128)(2,1)} %fusion.place_ref), custom_call_target="tpu_custom_call" | custom-call | tf_op jit(solution)/shard_map/fit/pallas_call | solution.py:317
  103.7 1.9 %reshape.258 = f32[8,1,12,8,96]{4,3,2,0,1:T(8,128)} reshape(f32[96,768]{1,0:T(8,128)} %fit.1) | data formatting | bytes 589824 | tf_op jit(solution)/shard_map/fit/reshape | solution.py:350
  (8 shorter events, 0.1 us)
Async XLA Ops:
  0.0 1.9 %copy-start = (bf16[4096,384]{1,0:T(8,128)(2,1)S(1)}, bf16[4096,384]{1,0:T(8,128)(2,1)}, u32[]{:S(2)}) copy-start(bf16[4096,384]{1,0:T(8,128)(2,1)} %param.10) | copy-start | bytes 9437188
  9.2 4.3 %copy-start.1 = (s32[32,2]{0,1:T(2,128)S(1)}, s32[32,2]{0,1:T(2,128)}, u32[]{:S(2)}) copy-start(s32[32,2]{0,1:T(2,128)} %param.7) | copy-start | bytes 772
  9.2 4.5 %copy-start.2 = (s32[8]{0:T(128)S(1)}, s32[8]{0:T(128)}, u32[]{:S(2)}) copy-start(s32[8]{0:T(128)} %param.11) | copy-start | bytes 100

commit v4 on v3

--- a/solution.py
+++ b/solution.py
@@ -190,9 +190,29 @@
             copy.wait_send()
 
 
-def pick_kernel(mine_ref, index_ref, left_ref, held, send_sem, recv_sem):
+def pick_kernel(
+    mine_ref, index_ref, wanted_ref, vir_ref, left_ref, rows_ref, place_ref,
+    held, windows, send_sem, recv_sem, window_sem,
+):
     owner, rank = lax.axis_index("aux"), lax.axis_index("occ")
-    ranks = held.shape[0]
+    plane, row = owner // ROWS, owner % ROWS
+    ranks, owners = held.shape[0], lax.axis_size("aux")
+    blocks, depth, columns = windows.shape
+    tall = vir_ref.shape[0] // owners
+    reads = []
+    for b, shift in enumerate(ring_order(blocks)):
+        source = lax.rem(plane + shift + blocks, blocks) * ROWS + row
+        for n, low in enumerate(range(0, depth, tall)):
+            size = min(tall, depth - low)
+            start = pl.multiple_of(lax.rem(source + n, owners) * tall, tall)
+            read = pltpu.make_async_copy(
+                vir_ref.at[pl.ds(start, size)],
+                windows.at[b, pl.ds(low, size)],
+                window_sem.at[b, n],
+            )
+            read.start()
+            reads.append(read)
+
     barrier = pltpu.get_barrier_semaphore()
     peers = [(owner, lax.rem(rank + r, ranks)) for r in range(1, ranks)]
     for peer in peers:
@@ -210,19 +230,39 @@
         )
         copy.start()
         copies.append(copy)
-    span = mine_ref.shape[1]
-    column = lax.broadcasted_iota(jnp.int32, (span, index_ref.shape[1]), 0)
-    total = None
-    for r in range(ranks):
-        if r > 0:
-            copies[r - 1].wait_recv()
-        first = lax.rem(rank + ranks - r, ranks) * span
-        hits = jnp.where(column == index_ref[...] - first, 1.0, 0.0).astype(jnp.bfloat16)
-        term = jnp.dot(
-            mine_ref[...] if r == 0 else held[r], hits, preferred_element_type=jnp.float32
-        )
-        total = term if total is None else total + term
-    left_ref[...] = total.astype(jnp.bfloat16)
+    held[0] = mine_ref[...]
+
+    place_ref[...] = jnp.where(
+        lax.broadcasted_iota(jnp.int32, place_ref.shape, 0) == wanted_ref[...], 1.0, 0.0
+    ).astype(jnp.bfloat16)
+    lanes = rows_ref.shape[2]
+    group = columns // owners * ROWS
+    source = lax.broadcasted_iota(jnp.int32, (2 * columns, lanes), 0)
+    target = lax.broadcasted_iota(jnp.int32, (2 * columns, lanes), 1)
+    half = lanes // 2
+    within = jnp.where(target < half, target, target - half)
+    first = jnp.where(target < half, 0, columns) + plane * group
+    hits = (source == first + within) & (within < group)
+    choose = jnp.where(hits, 1.0, 0.0).astype(jnp.bfloat16)
+    for read in reads:
+        read.wait()
+    for p in range(blocks // 2):
+        pair = jnp.concatenate([windows[2 * p], windows[2 * p + 1]], axis=1)
+        rows_ref[p] = jnp.dot(pair, choose, preferred_element_type=jnp.float32).astype(jnp.bfloat16)
+
+    for copy in copies:
+        copy.wait_recv()
+    each = mine_ref.shape[1] // tall
+    pieces = []
+    for n in range(3):
+        block = lax.rem(owner + n, owners)
+        slot = lax.rem(rank - block // each + ranks, ranks)
+        low = pl.multiple_of(lax.rem(block, each) * tall, tall)
+        pieces.append(held[slot, :, pl.ds(low, tall)])
+    near = jnp.concatenate(pieces, axis=1)
+    column = lax.broadcasted_iota(jnp.int32, (3 * tall, index_ref.shape[1]), 0)
+    named = jnp.where(column == index_ref[...], 1.0, 0.0).astype(jnp.bfloat16)
+    left_ref[...] = jnp.dot(near, named, preferred_element_type=jnp.float32).astype(jnp.bfloat16)
     for copy in copies:
         copy.wait_send()
 
@@ -257,35 +297,39 @@
     width = vir_group * ranks
     lane = 64
 
-    with jax.named_scope("vir_rows"):
-        cols = lax.dynamic_slice_in_dim(vir_coeff, plane * (ROWS * vir_group), ROWS * vir_group, 1)
-        cols = jnp.pad(cols, ((0, 0), (0, lane - ROWS * vir_group)))
-        cols = jnp.concatenate([cols, cols[:depth]], axis=0)
-        pieces = []
-        for shift in ring_order(planes):
-            source = ((plane + shift + planes) % planes) * ROWS + row
-            pieces.append(lax.dynamic_slice_in_dim(cols, source * (step * block_size), depth, 0))
-        vir_rows = jnp.stack(
-            [jnp.concatenate(pieces[b : b + 2], axis=1) for b in range(0, planes, 2)]
+    with jax.named_scope("places"):
+        target = jnp.arange(2 * ROWS * width, dtype=jnp.int32)[None, :]
+        wanted = (
+            slot_of(target // vir_group % ranks, rank, ranks) * (2 * lane)
+            + (target // (ROWS * width)) * lane
+            + ((target // width + row) % ROWS) * vir_group
+            + target % vir_group
         )
 
     with jax.named_scope("half"):
         picked = jnp.take(occ_coeff, batch_ids, axis=0)
-        index = blk_atoms[:, 0, None] * block_size + jnp.arange(block_size, dtype=jnp.int32)
+        first = (blk_atoms[:, 0, None] - owner * step + atom_total) % atom_total
+        index = first * block_size + jnp.arange(block_size, dtype=jnp.int32)
         vmem = pl.BlockSpec(memory_space=pltpu.VMEM)
         dma = pltpu.SemaphoreType.DMA
-        left = pl.pallas_call(
+        left, vir_rows, place = pl.pallas_call(
             pick_kernel,
-            out_shape=jax.ShapeDtypeStruct((batch, slots * block_size), jnp.bfloat16),
-            in_specs=[vmem] * 2,
-            out_specs=vmem,
+            out_shape=[
+                jax.ShapeDtypeStruct((batch, slots * block_size), jnp.bfloat16),
+                jax.ShapeDtypeStruct((planes // 2, depth, 2 * lane), jnp.bfloat16),
+                jax.ShapeDtypeStruct((ranks * 2 * lane, 2 * ROWS * width), jnp.bfloat16),
+            ],
+            in_specs=[vmem] * 3 + [pl.BlockSpec(memory_space=pl.ANY)],
+            out_specs=[vmem] * 3,
             scratch_shapes=[
                 pltpu.VMEM((ranks, *picked.shape), jnp.bfloat16),
+                pltpu.VMEM((planes, depth, vir_coeff.shape[1]), jnp.bfloat16),
                 dma((ranks,)),
                 dma((ranks,)),
+                dma((planes, 3)),
             ],
             compiler_params=pltpu.CompilerParams(collective_id=1, has_side_effects=True),
-        )(picked, index.reshape(1, slots * block_size))
+        )(picked, index.reshape(1, slots * block_size), wanted, vir_coeff)
         offset = (blk_atoms[:, 1] - owner * step + atom_total) % atom_total
         offset = jnp.where(jnp.arange(slots, dtype=jnp.int32) < blk_count[0], offset, -1)
         offset = jnp.repeat(offset, block_size)
@@ -301,15 +345,6 @@
         half = half.reshape(depth, batch * part)
 
     with jax.named_scope("fit"):
-        source = jnp.arange(ranks * 2 * lane, dtype=jnp.int32)[:, None]
-        target = jnp.arange(2 * ROWS * width, dtype=jnp.int32)[None, :]
-        wanted = (
-            slot_of(target // vir_group % ranks, rank, ranks) * (2 * lane)
-            + (target // (ROWS * width)) * lane
-            + ((target // width + row) % ROWS) * vir_group
-            + target % vir_group
-        )
-        place = (source == wanted).astype(jnp.bfloat16)
         total = batch * width
         kept = total // ranks
         piece = (width, batch * part)

time: 107 us -> 93 us (0.87)
  local copies, waits for them, and re-layouts: 14.9 us -> 6.72 us
  other arithmetic: 8.23 us -> 4.13 us
  matrix products: 2.18 us -> 0.59 us
    concatenate x2 -> x0, other arithmetic: 3.72 us -> none  [on_device(): cols = jnp.concatenate([cols, cols[:depth]], axis=0)]
    another operation x3 -> x0, other arithmetic: 1.89 us -> none  [on_device(): jnp.stack([jnp.concatenate(pieces[b:b + 2], axis=1) for b in range(0, pla...]
    unnamed x6 -> x4, local copies, waits for them, and re-layouts: 1.9 us -> 0.01 us
    convert_element_type x1 -> x0, other arithmetic: 1.78 us -> none  [on_device(): place = (source == wanted).astype(jnp.bfloat16)]
    dot_general x1, matrix products: 2.18 us -> 0.59 us  [on_device(): jnp.einsum('wik,knq->wniq', spread, mine.reshape(slots * block_size, bloc...]
    gather x1, local copies, waits for them, and re-layouts: 2.06 us -> 0.57 us  [on_device(): picked = jnp.take(occ_coeff, batch_ids, axis=0)]
    dynamic_slice x1, local copies, waits for them, and re-layouts: 3.63 us -> 2.26 us  [on_device(): mine = lax.dynamic_slice_in_dim(ints, rank * part, part, 3)]
    pad x1 -> x0, local copies, waits for them, and re-layouts: 1.18 us -> none  [on_device(): cols = jnp.pad(cols, ((0, 0), (0, lane - ROWS * vir_group)))]
where the time goes in v4:
time: 93 us; the launch traced here: 92.4 us
  Pallas kernels  80.1 us (86%)
  local copies, waits for them, and re-layouts  6.72 us (7%)
  other arithmetic  4.13 us (4%)
    pallas_call x1, Pallas kernels, on_device(): pl.pallas_call(exchange_kernel, out_shape=jax.ShapeDtypeStruct((kept, tot...  69.4 us
    pallas_call x1, Pallas kernels, on_device(): pl.pallas_call(pick_kernel, out_shape=[jax.ShapeDtypeStruct((batch, slots...  10.7 us
    dynamic_slice x1, local copies, waits for them, and re-layouts, on_device(): mine = lax.dynamic_slice_in_dim(ints, rank * part, part, 3)  2.26 us
    reshape x1, local copies, waits for them, and re-layouts, on_device(): return pair_ints.reshape(batch, 1, vir_group, batch, width)  1.9 us

profile of v4, /device:TPU:1, one launch (start us, length us, event | category | flops | bytes accessed | tf_op | source)
XLA Modules:
  0.0 92.4 jit_solution(8043235558157648183)
XLA Ops:
  0.0 0.0 copy-start
  0.8 0.7 compare_select_fusion.16
  1.5 0.7 fusion.27
  2.1 0.7 compare_and_fusion
  2.8 0.7 compare_select_fusion.11
  3.5 0.7 fusion.13.wanted_ref
  4.1 0.0 copy-done
  4.1 0.6 gather_fusion
  4.7 0.7 broadcast_select_fusion.mine_ref
  5.4 0.1 iota_add_fusion
  5.5 0.7 add.250.index_ref
  6.1 0.1 broadcast_in_dim.48
  6.2 0.1 eq.31
  6.3 10.7 %half.1 = (bf16[8,512]{1,0:T(8,128)(2,1)}, bf16[4,272,128]{2,1,0:T(8,128)(2,1)}, bf16[1024,768]{1,0:T(8,128)(2,1)}) custom-call(bf16[8,512]{1,0:T(8,128)(2,1)} %broadcast_select_fusion.mine_ref, s32[1,512]{1,0:T(1,128)} %add.250.index_ref, s32[1,768]{1,0:T(1,128)} %fusion.13.wanted_ref, bf16[4096,384]{1,0:T(8,128)(2,1)} %vir_ref.1), custom_call_target="tpu_custom_call" | custom-call | tf_op jit(solution)/shard_map/half/pallas_call | solution.py:315
  17.1 0.0 copy-start.1
  17.1 2.3 %constant_dynamic-slice_fusion = bf16[32,16,16,64]{3,2,1,0:T(8,128)(2,1)S(1)} fusion(bf16[32,16,16,512]{3,2,1,0:T(8,128)(2,1)} %param.6, s32[]{:T(128)S(6)} %select_n.169), kind=kLoop, calls=%fused_computation.67 | loop fusion | bytes 2097156 | tf_op jit(solution)/shard_map/half/dynamic_slice | solution.py:338
  19.3 0.0 copy-done.1
  19.3 0.6 fusion.5
  19.9 0.1 copy.11
  20.0 1.1 %reshape.460.half_ref = bf16[272,512]{1,0:T(8,128)(2,1)} reshape(bf16[17,16,8,64]{3,2,1,0:T(8,128)(2,1)S(1)} %copy.11) | data formatting | bytes 557056 | tf_op jit(solution)/shard_map/half/reshape | solution.py:345
  21.1 69.4 %fit.1 = f32[96,768]{1,0:T(8,128)} custom-call(bf16[4,272,128]{2,1,0:T(8,128)(2,1)} %get-tuple-element.8.vir_ref, bf16[272,512]{1,0:T(8,128)(2,1)} %reshape.460.half_ref, bf16[1024,768]{1,0:T(8,128)(2,1)} %get-tuple-element.10.place_ref), custom_call_target="tpu_custom_call" | custom-call | tf_op jit(solution)/shard_map/fit/pallas_call | solution.py:352
  90.5 1.9 %reshape.461 = f32[8,1,12,8,96]{4,3,2,0,1:T(8,128)} reshape(f32[96,768]{1,0:T(8,128)} %fit.1) | data formatting | bytes 589824 | tf_op jit(solution)/shard_map/fit/reshape | solution.py:385
  (2 shorter events, 0.0 us)
Async XLA Ops:
  0.0 4.1 %copy-start = (bf16[1280,512]{1,0:T(8,128)(2,1)S(1)}, bf16[1280,512]{1,0:T(8,128)(2,1)}, u32[]{:S(2)}) copy-start(bf16[1280,512]{1,0:T(8,128)(2,1)} %param.9) | copy-start | bytes 3932164
  17.1 2.3 %copy-start.1 = (bf16[8,512]{1,0:T(8,128)(2,1)S(1)}, bf16[8,512]{1,0:T(8,128)(2,1)}, u32[]{:S(2)}) copy-start(bf16[8,512]{1,0:T(8,128)(2,1)} %get-tuple-element.9) | copy-start | bytes 24580

commit v5 on v4

--- a/solution.py
+++ b/solution.py
@@ -68,38 +68,54 @@
             above if b % 2 else below,
         )
 
+    halves = ((0, after), (1, before))
+    cut = width // 2
+
+    def send_two_away(b):
+        for h, peer in halves:
+            some = pl.ds(cut * h, cut)
+            direct[b, 2, h] = send(
+                stage.at[b, 1, some], relay.at[b, some],
+                step_send.at[b, 2 + h], step_recv.at[b, 2 + h], peer,
+            )
+
     def pass_on(b):
-        direct[b, 2].wait_recv()
-        passed[b] = send(
-            relay.at[b], arrived.at[1, b], pass_send.at[b], pass_recv.at[b],
-            before if b % 2 else after,
-        )
-
-    def accumulate(p):
+        for h, peer in halves:
+            some = pl.ds(cut * h, cut)
+            direct[b, 2, h].wait_recv()
+            passed[b, h] = send(
+                relay.at[b, some], arrived.at[1, b, some],
+                pass_send.at[b, h], pass_recv.at[b, h], peer,
+            )
+
+    def accumulate(p, sources):
         first, second = 2 * p, 2 * p + 1
         for b in (first, second):
-            direct[b, 1].wait_recv()
-            direct[b, 3].wait_recv()
-            passed[b].wait_recv()
-        for r in range(ROWS):
+            for r in sources:
+                if r == 2:
+                    passed[b, 0].wait_recv()
+                    passed[b, 1].wait_recv()
+                elif r > 0:
+                    direct[b, r].wait_recv()
+        for n, r in enumerate(sources):
             for h in range(batch // 2):
                 cols = slice(2 * part * h, 2 * part * (h + 1))
                 if r == 0:
                     one, two = own[first, :, cols], own[second, :, cols]
                 else:
                     one, two = arrived[r - 1, first, :, cols], arrived[r - 1, second, :, cols]
-                place = slice(2 * part * r, 2 * part * (r + 1))
+                place = slice(2 * part * n, 2 * part * (n + 1))
                 rows[width * 2 * h : width * (2 * h + 1), place] = jnp.concatenate(
                     [one[:, :part], two[:, :part]], axis=1
                 )
                 rows[width * (2 * h + 1) : width * (2 * h + 2), place] = jnp.concatenate(
                     [one[:, part:], two[:, part:]], axis=1
                 )
-        half = rows.shape[0] // 2
+        half, used = rows.shape[0] // 2, 2 * part * len(sources)
         for t in range(2):
             product = lax.dot_general(
-                rows[half * t : half * (t + 1)],
-                rows[...],
+                rows[half * t : half * (t + 1), :used],
+                rows[:, :used],
                 (((1,), (1,)), ((), ())),
                 preferred_element_type=jnp.float32,
             )
@@ -140,24 +156,22 @@
         own[b] = summed[:width]
         for r in range(1, ROWS):
             stage[b, r - 1] = summed[width * r : width * (r + 1)]
+        send_two_away(b)
         direct[b, 1] = send(
             stage.at[b, 0], arrived.at[0, b], step_send.at[b, 0], step_recv.at[b, 0], after
         )
         direct[b, 3] = send(
-            stage.at[b, 2], arrived.at[2, b], step_send.at[b, 2], step_recv.at[b, 2], before
-        )
-        direct[b, 2] = send(
-            stage.at[b, 1], relay.at[b], step_send.at[b, 1], step_recv.at[b, 1],
-            before if b % 2 else after,
+            stage.at[b, 2], arrived.at[2, b], step_send.at[b, 1], step_recv.at[b, 1], before
         )
         if b > 0:
             pass_on(b - 1)
         if b % 2 and (b + 1) // 2 < parts:
             pass_vir((b + 1) // 2)
         if b % 2 and b > 2:
-            accumulate((b - 3) // 2)
+            accumulate((b - 3) // 2, (0, 1, 3, 2))
     pass_on(blocks - 1)
-    accumulate(blocks // 2 - 1)
+    accumulate(blocks // 2 - 1, (0, 1, 3))
+    accumulate(blocks // 2 - 1, (2,))
 
     kept = width // ranks
     for a in range(ranks):
@@ -166,7 +180,7 @@
                 width * i + kept * a : width * i + kept * (a + 1)
             ]
     chip = rank // 2
-    order = [*range(1, chips), 0]
+    order = [chips // 2, *(k for k in range(1, chips) if k != chips // 2), 0]
     for k in order:
         theirs = 2 * lax.rem(chip + k, chips) + 1 - core
         joins[k] = send(
@@ -371,10 +385,10 @@
                 dma((planes // 2, ranks - 1)),
                 dma((planes - 1,)),
                 dma((planes - 1,)),
-                dma((planes, ROWS - 1)),
-                dma((planes, ROWS - 1)),
-                dma((planes,)),
-                dma((planes,)),
+                dma((planes, ROWS)),
+                dma((planes, ROWS)),
+                dma((planes, 2)),
+                dma((planes, 2)),
                 dma((chips,)),
                 dma((chips,)),
                 dma((chips - 1,)),

time: 93 us -> 89.1 us (0.958)
  Pallas kernels: 80.1 us -> 76.5 us
    pallas_call x1, Pallas kernels: 69.4 us -> 65.8 us  [on_device(): pl.pallas_call(exchange_kernel, out_shape=jax.ShapeDtypeStruct((kept, tot...]
where the time goes in v5:
time: 89.1 us; the launch traced here: 88.8 us
  Pallas kernels  76.5 us (86%)
  local copies, waits for them, and re-layouts  6.72 us (8%)
  other arithmetic  4.13 us (5%)
    pallas_call x1, Pallas kernels, on_device(): pl.pallas_call(exchange_kernel, out_shape=jax.ShapeDtypeStruct((kept, tot...  65.8 us
    pallas_call x1, Pallas kernels, on_device(): pl.pallas_call(pick_kernel, out_shape=[jax.ShapeDtypeStruct((batch, slots...  10.7 us
    dynamic_slice x1, local copies, waits for them, and re-layouts, on_device(): mine = lax.dynamic_slice_in_dim(ints, rank * part, part, 3)  2.26 us
    reshape x1, local copies, waits for them, and re-layouts, on_device(): return pair_ints.reshape(batch, 1, vir_group, batch, width)  1.9 us

profile of v5, /device:TPU:1, one launch (start us, length us, event | category | flops | bytes accessed | tf_op | source)
XLA Modules:
  0.0 88.8 jit_solution(17214412009639324881)
XLA Ops:
  0.0 0.0 copy-start
  0.8 0.7 compare_select_fusion.16
  1.5 0.7 fusion.27
  2.1 0.7 compare_and_fusion
  2.8 0.7 compare_select_fusion.11
  3.5 0.7 fusion.13.wanted_ref
  4.1 0.0 copy-done
  4.1 0.6 gather_fusion
  4.7 0.7 broadcast_select_fusion.mine_ref
  5.4 0.1 iota_add_fusion
  5.5 0.7 add.250.index_ref
  6.1 0.1 broadcast_in_dim.48
  6.2 0.1 eq.31
  6.3 10.7 %half.1 = (bf16[8,512]{1,0:T(8,128)(2,1)}, bf16[4,272,128]{2,1,0:T(8,128)(2,1)}, bf16[1024,768]{1,0:T(8,128)(2,1)}) custom-call(bf16[8,512]{1,0:T(8,128)(2,1)} %broadcast_select_fusion.mine_ref, s32[1,512]{1,0:T(1,128)} %add.250.index_ref, s32[1,768]{1,0:T(1,128)} %fusion.13.wanted_ref, bf16[4096,384]{1,0:T(8,128)(2,1)} %vir_ref.1), custom_call_target="tpu_custom_call" | custom-call | tf_op jit(solution)/shard_map/half/pallas_call | solution.py:329
  17.1 0.0 copy-start.1
  17.1 2.3 %constant_dynamic-slice_fusion = bf16[32,16,16,64]{3,2,1,0:T(8,128)(2,1)S(1)} fusion(bf16[32,16,16,512]{3,2,1,0:T(8,128)(2,1)} %param.6, s32[]{:T(128)S(6)} %select_n.169), kind=kLoop, calls=%fused_computation.67 | loop fusion | bytes 2097156 | tf_op jit(solution)/shard_map/half/dynamic_slice | solution.py:352
  19.3 0.0 copy-done.1
  19.3 0.6 fusion.5
  19.9 0.1 copy.11
  20.0 1.1 %reshape.460.half_ref = bf16[272,512]{1,0:T(8,128)(2,1)} reshape(bf16[17,16,8,64]{3,2,1,0:T(8,128)(2,1)S(1)} %copy.11) | data formatting | bytes 557056 | tf_op jit(solution)/shard_map/half/reshape | solution.py:359
  21.1 65.8 %fit.1 = f32[96,768]{1,0:T(8,128)} custom-call(bf16[4,272,128]{2,1,0:T(8,128)(2,1)} %get-tuple-element.8.vir_ref, bf16[272,512]{1,0:T(8,128)(2,1)} %reshape.460.half_ref, bf16[1024,768]{1,0:T(8,128)(2,1)} %get-tuple-element.10.place_ref), custom_call_target="tpu_custom_call" | custom-call | tf_op jit(solution)/shard_map/fit/pallas_call | solution.py:366
  86.9 1.9 %reshape.461 = f32[8,1,12,8,96]{4,3,2,0,1:T(8,128)} reshape(f32[96,768]{1,0:T(8,128)} %fit.1) | data formatting | bytes 589824 | tf_op jit(solution)/shard_map/fit/reshape | solution.py:399
  (2 shorter events, 0.0 us)
Async XLA Ops:
  0.0 4.1 %copy-start = (bf16[1280,512]{1,0:T(8,128)(2,1)S(1)}, bf16[1280,512]{1,0:T(8,128)(2,1)}, u32[]{:S(2)}) copy-start(bf16[1280,512]{1,0:T(8,128)(2,1)} %param.9) | copy-start | bytes 3932164
  17.1 2.3 %copy-start.1 = (bf16[8,512]{1,0:T(8,128)(2,1)S(1)}, bf16[8,512]{1,0:T(8,128)(2,1)}, u32[]{:S(2)}) copy-start(bf16[8,512]{1,0:T(8,128)(2,1)} %get-tuple-element.9) | copy-start | bytes 24580

commit v6 on v5

--- a/solution.py
+++ b/solution.py
@@ -132,10 +132,10 @@
         send_vir(p, 0, 1, vir_ref.at[p], partner)
     pass_vir(0)
     for b in range(blocks):
-        if b > 0:
-            ring[b].wait_recv()
-            if b + 2 < blocks:
-                send_ring(b + 2, held.at[b - 1])
+        for c in range(b, min(b + 2, blocks)) if b % 2 else ():
+            ring[c].wait_recv()
+            if c + 2 < blocks:
+                send_ring(c + 2, held.at[c - 1])
         if b % 2 == 0:
             p = b // 2
             for k in range(chips):

time: 89.1 us -> 89.2 us (level)
  no operation moved by 1% of the time
where the time goes in v6:
time: 89.2 us; the launch traced here: 89 us
  Pallas kernels  76.7 us (86%)
  local copies, waits for them, and re-layouts  6.72 us (8%)
  other arithmetic  4.13 us (5%)
    pallas_call x1, Pallas kernels, on_device(): pl.pallas_call(exchange_kernel, out_shape=jax.ShapeDtypeStruct((kept, tot...  66 us
    pallas_call x1, Pallas kernels, on_device(): pl.pallas_call(pick_kernel, out_shape=[jax.ShapeDtypeStruct((batch, slots...  10.7 us
    dynamic_slice x1, local copies, waits for them, and re-layouts, on_device(): mine = lax.dynamic_slice_in_dim(ints, rank * part, part, 3)  2.26 us
    reshape x1, local copies, waits for them, and re-layouts, on_device(): return pair_ints.reshape(batch, 1, vir_group, batch, width)  1.9 us

profile of v6, /device:TPU:1, one launch (start us, length us, event | category | flops | bytes accessed | tf_op | source)
XLA Modules:
  0.0 89.0 jit_solution(3075815342612526186)
XLA Ops:
  0.0 0.0 copy-start
  0.8 0.7 compare_select_fusion.16
  1.5 0.7 fusion.27
  2.1 0.7 compare_and_fusion
  2.8 0.7 compare_select_fusion.11
  3.5 0.7 fusion.13.wanted_ref
  4.1 0.0 copy-done
  4.1 0.6 gather_fusion
  4.7 0.7 broadcast_select_fusion.mine_ref
  5.4 0.1 iota_add_fusion
  5.5 0.7 add.250.index_ref
  6.1 0.1 broadcast_in_dim.48
  6.2 0.1 eq.31
  6.3 10.7 %half.1 = (bf16[8,512]{1,0:T(8,128)(2,1)}, bf16[4,272,128]{2,1,0:T(8,128)(2,1)}, bf16[1024,768]{1,0:T(8,128)(2,1)}) custom-call(bf16[8,512]{1,0:T(8,128)(2,1)} %broadcast_select_fusion.mine_ref, s32[1,512]{1,0:T(1,128)} %add.250.index_ref, s32[1,768]{1,0:T(1,128)} %fusion.13.wanted_ref, bf16[4096,384]{1,0:T(8,128)(2,1)} %vir_ref.1), custom_call_target="tpu_custom_call" | custom-call | tf_op jit(solution)/shard_map/half/pallas_call | solution.py:329
  17.1 0.0 copy-start.1
  17.1 2.3 %constant_dynamic-slice_fusion = bf16[32,16,16,64]{3,2,1,0:T(8,128)(2,1)S(1)} fusion(bf16[32,16,16,512]{3,2,1,0:T(8,128)(2,1)} %param.6, s32[]{:T(128)S(6)} %select_n.169), kind=kLoop, calls=%fused_computation.67 | loop fusion | bytes 2097156 | tf_op jit(solution)/shard_map/half/dynamic_slice | solution.py:352
  19.3 0.0 copy-done.1
  19.3 0.6 fusion.5
  19.9 0.1 copy.11
  20.0 1.1 %reshape.460.half_ref = bf16[272,512]{1,0:T(8,128)(2,1)} reshape(bf16[17,16,8,64]{3,2,1,0:T(8,128)(2,1)S(1)} %copy.11) | data formatting | bytes 557056 | tf_op jit(solution)/shard_map/half/reshape | solution.py:359
  21.1 66.0 %fit.1 = f32[96,768]{1,0:T(8,128)} custom-call(bf16[4,272,128]{2,1,0:T(8,128)(2,1)} %get-tuple-element.8.vir_ref, bf16[272,512]{1,0:T(8,128)(2,1)} %reshape.460.half_ref, bf16[1024,768]{1,0:T(8,128)(2,1)} %get-tuple-element.10.place_ref), custom_call_target="tpu_custom_call" | custom-call | tf_op jit(solution)/shard_map/fit/pallas_call | solution.py:366
  87.1 1.9 %reshape.461 = f32[8,1,12,8,96]{4,3,2,0,1:T(8,128)} reshape(f32[96,768]{1,0:T(8,128)} %fit.1) | data formatting | bytes 589824 | tf_op jit(solution)/shard_map/fit/reshape | solution.py:399
  (2 shorter events, 0.0 us)
Async XLA Ops:
  0.0 4.1 %copy-start = (bf16[1280,512]{1,0:T(8,128)(2,1)S(1)}, bf16[1280,512]{1,0:T(8,128)(2,1)}, u32[]{:S(2)}) copy-start(bf16[1280,512]{1,0:T(8,128)(2,1)} %param.9) | copy-start | bytes 3932164
  17.1 2.3 %copy-start.1 = (bf16[8,512]{1,0:T(8,128)(2,1)S(1)}, bf16[8,512]{1,0:T(8,128)(2,1)}, u32[]{:S(2)}) copy-start(bf16[8,512]{1,0:T(8,128)(2,1)} %get-tuple-element.9) | copy-start | bytes 24580
